TPU v7x, 128 devices: a whole 4x4x4 slice. The times are simulated.
128 devices in a mesh: section: 2 (over core), dp: 16 (over y, x), mp: 4 (over z).
Axes of the slice: x: 4, y: 4, z: 4, core: 2. Of those that a mesh axis runs over, the one named last changes fastest.
Arguments:
- patches: bfloat16 [8192, 1280], P(('section', 'dp', 'mp')), may hold values from -6 to 6
- image_units: int32 [128, 3], P(('section', 'dp', 'mp')), may hold values from 1 to 8, 16 in all within a row
- v_gain: float32 [1280], replicated, may hold values from 0.5 to 1.5
- v_qkv: bfloat16 [1280, 3840], replicated, may hold values from -0.15625 to 0.15625
- v_out: bfloat16 [1280, 1280], replicated, may hold values from -0.15625 to 0.15625
- merge_gain: float32 [1280], replicated, may hold values from 0.5 to 1.5
- w_merge: bfloat16 [5120, 8192], P('dp', 'mp'), may hold values from -0.078125 to 0.078125
- routes: int32 [2048, 1], P(('section', 'dp', 'mp')), may hold values from 0 to 15; in each aligned block of 1024 rows (0 to 1023, 1024 to 2047, ...) at most 128 rows name the same one
- text: bfloat16 [4096, 8192], P(('section', 'dp'), 'mp'), may hold values from -6 to 6
- seq_lengths: int32 [32, 3], P(('section', 'dp')), may hold values from 1 to 64, 128 in all within a row
- lang_gain: float32 [2, 8192], P('section'), may hold values from 0.5 to 1.5
- w_qkv: bfloat16 [2, 8192, 5120], P('section', 'dp', 'mp'), may hold values from -0.0625 to 0.0625
- wo_t: bfloat16 [2, 8192, 4096], P('section', 'dp', 'mp'), may hold values from -0.09375 to 0.09375
- row_grads: bfloat16 [4096, 8192], P(('section', 'dp'), 'mp'), may hold values from -6 to 6
Outputs:
- final_hidden: bfloat16 [4096, 8192], P(('section', 'dp'), 'mp')
- merged_grads: bfloat16 [2048, 8192], P(('section', 'dp', 'mp'))
Inputs may be any that keep to these rules, and one draw needn't show every extreme that they name: `image_units`: each row sums to 16. `routes`: among the 1024 rows of one section index (aligned blocks), at most 128 name one group; in some section index one group is named by exactly 128. `seq_lengths`: each row sums to 128.
All inputs are finite; a program needn't handle non-finite values.
Results may differ from a plain program's by a relative error of at most 0.03.
Values may be sent and summed in bfloat16 or wider, within the bound.
A program may use at most 192 MiB of HBM per device.

v0:
```python
import math

import jax
import jax.numpy as jnp
from jax import lax
from jax.sharding import PartitionSpec as P

QH = 32
KVH = 4
HD = 128
VD = 1280
VH = 16
VHD = 80
MERGE = 4


EPSILON = 1e-06


def passed_along(value, axis, steps):
    count = lax.axis_size(axis)
    initial, last = (max(0, -steps), min(count, count - steps))
    return lax.ppermute(value, axis, [(source, source + steps) for source in range(initial, last)])


def broadcast(block, axis, owner):
    block = jnp.where(lax.axis_index(axis) == owner, block, jnp.zeros_like(block))
    return lax.psum(block, axis)


def layer_norm(values, norm_gain):
    values = values.astype(jnp.float32)
    centre = jnp.mean(values, axis=-1, keepdims=True)
    centred = values - centre
    variance = jnp.mean(centred * centred, axis=-1, keepdims=True)
    return centred * lax.rsqrt(variance + EPSILON) * norm_gain


def rms_norm(values, norm_gain):
    values = values.astype(jnp.float32)
    return (
        values * lax.rsqrt(jnp.mean(values * values, axis=-1, keepdims=True) + EPSILON) * norm_gain
    )


def segment_of(lengths, amount):
    boundary = jnp.cumsum(lengths.astype(jnp.int32))
    positions = jnp.arange(amount, dtype=jnp.int32)
    return jnp.sum((positions[:, None] >= boundary[None, :]).astype(jnp.int32), axis=1)


def vision_rows(patches, units, v_gain, v_qkv, v_out, merge_gain):
    amount = patches.shape[0]
    merged_count = amount // MERGE
    unit_image = segment_of(units, merged_count)
    image_ids = jnp.broadcast_to(unit_image[:, None], (merged_count, MERGE)).reshape(amount)
    v_normed = layer_norm(patches, v_gain).astype(jnp.bfloat16)
    projected = jnp.dot(v_normed, v_qkv, preferred_element_type=jnp.float32).astype(jnp.bfloat16)
    projected = projected.reshape(amount, 3, VH, VHD)
    scores = jnp.einsum(
        "qhd,khd->hqk", projected[:, 0], projected[:, 1], preferred_element_type=jnp.float32
    ) / math.sqrt(VHD)
    allowed = image_ids[:, None] == image_ids[None, :]
    scores = jnp.where(allowed[None], scores, -1e30)
    weights = jax.nn.softmax(scores, axis=-1).astype(jnp.bfloat16)
    attended = (
        jnp.einsum("hqk,khd->qhd", weights, projected[:, 2], preferred_element_type=jnp.float32)
        .astype(jnp.bfloat16)
        .reshape(amount, VD)
    )
    update = jnp.dot(attended, v_out, preferred_element_type=jnp.float32)
    v_hidden = (patches.astype(jnp.float32) + update).astype(jnp.bfloat16)
    merged = layer_norm(v_hidden, merge_gain).astype(jnp.bfloat16)
    return merged.reshape(merged_count, MERGE * VD)


def attend(projected, lengths):
    seq_rows = projected.shape[0]
    group_size = QH // KVH
    kv_here = projected.shape[1] // ((group_size + 2) * HD)
    heads_view = projected.reshape(seq_rows, kv_here, group_size + 2, HD)
    scores = jnp.einsum(
        "tkgd,skd->kgts",
        heads_view[:, :, :group_size],
        heads_view[:, :, group_size],
        preferred_element_type=jnp.float32,
    ) * (1.0 / math.sqrt(HD))
    seq_ids = segment_of(lengths, seq_rows)
    positions = jnp.arange(seq_rows, dtype=jnp.int32)
    allowed = (seq_ids[:, None] == seq_ids[None, :]) & (positions[:, None] >= positions[None, :])
    scores = jnp.where(allowed[None, None], scores, -1e30)
    weights = jax.nn.softmax(scores, axis=-1).astype(jnp.bfloat16)
    attended = jnp.einsum(
        "kgts,skd->tkgd",
        weights,
        heads_view[:, :, group_size + 1],
        preferred_element_type=jnp.float32,
    ).astype(jnp.bfloat16)
    return attended.reshape(seq_rows, kv_here * group_size * HD)


def shards(
    patches,
    image_units,
    v_gain,
    v_qkv,
    v_out,
    merge_gain,
    w_merge,
    routes,
    text,
    seq_lengths,
    lang_gain,
    w_qkv,
    wo_t,
    row_grads,
):
    merged = vision_rows(patches, image_units[0], v_gain, v_qkv, v_out, merge_gain)
    all_rows, all_routes = (
        lax.all_gather(merged, ("dp", "mp"), axis=0, tiled=True),
        lax.all_gather(routes, ("dp", "mp"), axis=0, tiled=True),
    )
    target = all_routes[:, 0]
    section_rows = target.shape[0]
    row_order = jnp.arange(section_rows, dtype=jnp.int32)
    matching = target[:, None] == target[None, :]
    position = jnp.sum(
        (matching & (row_order[:, None] > row_order[None, :])).astype(jnp.int32), axis=1
    )
    seq_rows = text.shape[0]
    slot_index = target * seq_rows + position
    group_here = lax.axis_index("dp")
    dp_count = lax.axis_size("dp")
    slice_width = w_merge.shape[0]
    row_slice = lax.dynamic_slice_in_dim(all_rows, group_here * slice_width, slice_width, 1)
    wanted = jnp.arange(seq_rows * lax.axis_size("dp"), dtype=jnp.int32)
    picker = (slot_index[None, :] == wanted[:, None]).astype(jnp.bfloat16)
    picked = jnp.dot(picker, row_slice, preferred_element_type=jnp.float32).astype(jnp.bfloat16)
    image_rows = lax.psum_scatter(
        jnp.dot(picked, w_merge, preferred_element_type=jnp.float32).astype(jnp.bfloat16),
        "dp",
        scatter_dimension=0,
        tiled=True,
    )
    present = jnp.sum((target == group_here).astype(jnp.int32))
    positions = jnp.arange(seq_rows, dtype=jnp.int32)
    entry_rows = jnp.where((positions < present)[:, None], image_rows, text)
    gathered = (
        lax.all_gather(w_qkv, "dp", axis=1, tiled=True),
        lax.all_gather(wo_t, "dp", axis=1, tiled=True),
    )
    qkv_weight = gathered[0][0]
    out_weight = gathered[1][0]
    norm_gain = lang_gain[0]
    sections = lax.axis_size("section")
    section_here = lax.axis_index("section")
    is_first = section_here == 0
    lengths_here = seq_lengths[0]
    entry_all, lengths_all = (
        lax.all_gather(entry_rows, "section", axis=0, tiled=True),
        lax.all_gather(seq_lengths, "section", axis=0, tiled=True),
    )
    carried = jnp.zeros_like(entry_rows)
    carried_lengths = lengths_here
    finished = []
    for section_step in range(2 * sections - 1):
        if section_step > 0:
            carried, carried_lengths = passed_along((carried, carried_lengths), "section", 1)
        if section_step < sections:
            incoming = entry_all[section_step * seq_rows : (section_step + 1) * seq_rows]
            incoming_lengths = lengths_all[section_step]
            carried = jnp.where(is_first, incoming, carried)
            carried_lengths = jnp.where(is_first, incoming_lengths, carried_lengths)
        features = lax.all_gather(carried, "mp", axis=1, tiled=True)
        normed = rms_norm(features, norm_gain).astype(jnp.bfloat16)
        projected = jnp.dot(normed, qkv_weight, preferred_element_type=jnp.float32)
        attended = attend(projected.astype(jnp.bfloat16), carried_lengths)
        partial_value = lax.dot_general(
            attended, out_weight, (((1,), (1,)), ((), ())), preferred_element_type=jnp.float32
        )
        update = lax.psum_scatter(
            partial_value.astype(jnp.bfloat16), "mp", scatter_dimension=1, tiled=True
        ).astype(jnp.float32)
        carried = (carried.astype(jnp.float32) + update).astype(jnp.bfloat16)
        if section_step >= sections - 1:
            finished.append(carried)
    returned_rows = broadcast(jnp.stack(finished), "section", sections - 1)
    final_hidden = lax.dynamic_index_in_dim(returned_rows, section_here, 0, keepdims=False)
    columns = row_grads.shape[1]
    picker = ((target == group_here)[:, None] & (position[:, None] == positions[None, :])).astype(
        jnp.bfloat16
    )
    outgoing = jnp.dot(picker, row_grads, preferred_element_type=jnp.float32).astype(jnp.bfloat16)
    outgoing = outgoing.reshape(dp_count, section_rows // dp_count, columns)
    returned = lax.all_to_all(
        lax.all_to_all(outgoing, "dp", split_axis=0, concat_axis=0, tiled=True),
        "mp",
        split_axis=1,
        concat_axis=2,
        tiled=True,
    )
    merged_grads = jnp.sum(returned.astype(jnp.float32), axis=0).astype(jnp.bfloat16)
    return (final_hidden, merged_grads)


def solution(mesh):
    in_specs = (
        P(("section", "dp", "mp"), None),
        P(("section", "dp", "mp"), None),
        P(),
        P(),
        P(),
        P(),
        P("dp", "mp"),
        P(("section", "dp", "mp"), None),
        P(("section", "dp"), "mp"),
        P(("section", "dp"), None),
        P("section", None),
        P("section", "dp", "mp"),
        P("section", "dp", "mp"),
        P(("section", "dp"), "mp"),
    )
    out_specs = (P(("section", "dp"), "mp"), P(("section", "dp", "mp"), None))
    return jax.shard_map(shards, mesh=mesh, in_specs=in_specs, out_specs=out_specs, check_vma=False)
```

profile of v0, /device:TPU:0, one launch (start us, length us, event | category | flops | bytes accessed | tf_op | source)
XLA Modules:
  0.0 799.9 jit_solution(8067572202809848577)
XLA Ops:
  9.6 6.6 convolution_convert_fusion.1
  34.4 24.9 %all-reduce = s32[1024]{0:T(1024)S(1)} all-reduce(s32[1024]{0:T(1024)S(1)} %bitcast_dynamic-update-slice_fusion), channel_id=1, replica_groups=mesh['section'=2,'dp'=16,'mp'=4] {'dp','mp'}, use_global_device_ids=true, to_apply=%add | all-reduce | flops 1024 | bytes 8192 | tf_op jit(solution)/shard_map/squeeze | solution.py:123
  60.4 60.5 %all-gather.9.cloned.1.call-done = bf16[1024,5120]{1,0:T(8,128)(2,1)} async-done(((bf16[16,5120]{1,0:T(8,128)(2,1)}), bf16[1024,5120]{1,0:T(8,128)(2,1)}) %all-gather.9.cloned.1.call-update) | async-done | bytes 10485776 | tf_op jit(solution)/shard_map/all_gather | solution.py:120
  120.9 10.7 %convolution_convert_fusion = bf16[2048,2048]{1,0:T(8,128)(2,1)} fusion(bf16[320,2048]{1,0:T(8,128)(2,1)} %param.20, s32[1024]{0:T(1024)S(1)} %get-tuple-element.7, bf16[1024,5120]{1,0:T(8,128)(2,1)} %all-gather.9.cloned.1.call-done, s32[]{:T(128)S(6)} %select_n.69), kind=kOutput, calls=%fused_computation.18 | convolution fusion | flops 4033478656 | bytes 10489860 | tf_op jit(solution)/shard_map/dot_general | solution.py:140
  132.4 83.9 %reduce-scatter.5.cloned.1.call-done = bf16[128,2048]{1,0:T(8,128)(2,1)} async-done(((bf16[2048,2048]{1,0:T(8,128)(2,1)}), bf16[128,2048]{1,0:T(8,128)(2,1)}) %reduce-scatter.5.cloned.1.call-update) | async-done | bytes 524304 | tf_op jit(solution)/shard_map/reduce_scatter | solution.py:139
  218.4 11.4 %all-gather.11.cloned.1.call-done = bf16[256,2048]{1,0:T(8,128)(2,1)} async-done(((bf16[128,2048]{1,0:T(8,128)(2,1)}), bf16[256,2048]{1,0:T(8,128)(2,1)}) %all-gather.11.cloned.1.call-update) | async-done | bytes 1048592 | tf_op jit(solution)/shard_map/all_gather | solution.py:160
  235.2 29.1 %all-gather.13.cloned.1.call-done = bf16[128,8192]{1,0:T(8,128)(2,1)} async-done(((bf16[128,2048]{1,0:T(8,128)(2,1)}), bf16[128,8192]{1,0:T(8,128)(2,1)}) %all-gather.13.cloned.1.call-update) | async-done | bytes 2097168 | tf_op jit(solution)/shard_map/all_gather | solution.py:174
  266.4 132.4 %all-gather.15.cloned.1.call-done = bf16[1,8192,1280]{2,1,0:T(8,128)(2,1)} async-done(((bf16[1,512,1280]{2,1,0:T(8,128)(2,1)}), bf16[1,8192,1280]{2,1,0:T(8,128)(2,1)}) %all-gather.15.cloned.1.call-update) | async-done | bytes 20971536 | tf_op jit(solution)/shard_map/all_gather | solution.py:149
  398.8 10.6 %fusion.35 = bf16[128,1280]{1,0:T(8,128)(2,1)S(1)} fusion(bf16[1,8192,1280]{2,1,0:T(8,128)(2,1)} %all-gather.15.cloned.1.call-done, bf16[128,8192]{1,0:T(8,128)(2,1)} %all-gather.13.cloned.1.call-done, f32[8192]{0:T(1024)S(1)} %bitcast.203, f32[128]{0:T(128)S(1)} %add_rsqrt_fusion.2), kind=kOutput, calls=%fused_computation.41 | convolution fusion | flops 2688712704 | bytes 23429632 | tf_op jit(solution)/shard_map/dot_general | solution.py:176
  410.2 101.6 %all-gather.17.cloned.1.call-done = bf16[1,8192,1024]{2,1,0:T(8,128)(2,1)} async-done(((bf16[1,512,1024]{2,1,0:T(8,128)(2,1)}), bf16[1,8192,1024]{2,1,0:T(8,128)(2,1)}) %all-gather.17.cloned.1.call-update) | async-done | bytes 16777232 | tf_op jit(solution)/shard_map/all_gather | solution.py:150
  511.8 12.8 %fusion.13 = bf16[128,8192]{1,0:T(8,128)(2,1)} fusion(bf16[128,1024]{0,1:T(8,128)(2,1)S(1)} %bitcast.197, bf16[1,8192,1024]{2,1,0:T(8,128)(2,1)} %all-gather.17.cloned.1.call-done), kind=kOutput, calls=%fused_computation.13 | convolution fusion | flops 2148532224 | bytes 19136512 | tf_op jit(solution)/shard_map/dot_general | solution.py:178
  524.7 29.7 %reduce-scatter.7.cloned.1.call-done = bf16[128,2048]{1,0:T(8,128)(2,1)} async-done(((bf16[128,8192]{1,0:T(8,128)(2,1)}), bf16[128,2048]{1,0:T(8,128)(2,1)}) %reduce-scatter.7.cloned.1.call-update) | async-done | bytes 524304 | tf_op jit(solution)/shard_map/reduce_scatter | solution.py:181
  563.3 27.3 %all-gather.19.cloned.1.call-done = bf16[128,8192]{1,0:T(8,128)(2,1)} async-done(((bf16[128,2048]{1,0:T(8,128)(2,1)}), bf16[128,8192]{1,0:T(8,128)(2,1)}) %all-gather.19.cloned.1.call-update) | async-done | bytes 2097168 | tf_op jit(solution)/shard_map/all_gather | solution.py:174
  592.7 10.6 %fusion.38 = bf16[128,1280]{1,0:T(8,128)(2,1)S(1)} fusion(bf16[1,8192,1280]{2,1,0:T(8,128)(2,1)} %all-gather.15.cloned.1.call-done, bf16[128,8192]{1,0:T(8,128)(2,1)} %all-gather.19.cloned.1.call-done, f32[128]{0:T(128)S(1)} %add_rsqrt_fusion.1, f32[8192]{0:T(1024)S(1)} %bitcast.204), kind=kOutput, calls=%fused_computation.42 | convolution fusion | flops 2688712704 | bytes 23429632 | tf_op jit(solution)/shard_map/dot_general | solution.py:176
  604.1 12.8 %fusion.16 = bf16[128,8192]{1,0:T(8,128)(2,1)} fusion(bf16[128,1024]{0,1:T(8,128)(2,1)S(1)} %bitcast.199, bf16[1,8192,1024]{2,1,0:T(8,128)(2,1)} %all-gather.17.cloned.1.call-done), kind=kOutput, calls=%fused_computation.14 | convolution fusion | flops 2148532224 | bytes 19136512 | tf_op jit(solution)/shard_map/dot_general | solution.py:178
  617.0 29.9 %reduce-scatter.9.cloned.1.call-done = bf16[128,2048]{1,0:T(8,128)(2,1)} async-done(((bf16[128,8192]{1,0:T(8,128)(2,1)}), bf16[128,2048]{1,0:T(8,128)(2,1)}) %reduce-scatter.9.cloned.1.call-update) | async-done | bytes 524304 | tf_op jit(solution)/shard_map/reduce_scatter | solution.py:181
  655.3 6.9 all-to-all-start
  665.4 17.6 %all-gather.21.cloned.1.call-done = bf16[128,8192]{1,0:T(8,128)(2,1)} async-done(((bf16[128,2048]{1,0:T(8,128)(2,1)}), bf16[128,8192]{1,0:T(8,128)(2,1)}) %all-gather.21.cloned.1.call-update) | async-done | bytes 2097168 | tf_op jit(solution)/shard_map/all_gather | solution.py:174
  685.1 10.6 %fusion.41 = bf16[128,1280]{1,0:T(8,128)(2,1)S(1)} fusion(bf16[1,8192,1280]{2,1,0:T(8,128)(2,1)} %all-gather.15.cloned.1.call-done, bf16[128,8192]{1,0:T(8,128)(2,1)} %all-gather.21.cloned.1.call-done, f32[128]{0:T(128)S(1)} %add_rsqrt_fusion, f32[8192]{0:T(1024)S(1)} %bitcast.205), kind=kOutput, calls=%fused_computation.43 | convolution fusion | flops 2688712704 | bytes 23429632 | tf_op jit(solution)/shard_map/dot_general | solution.py:176
  696.6 12.8 %fusion.19 = bf16[128,8192]{1,0:T(8,128)(2,1)} fusion(bf16[128,1024]{0,1:T(8,128)(2,1)S(1)} %bitcast.198, bf16[1,8192,1024]{2,1,0:T(8,128)(2,1)} %all-gather.17.cloned.1.call-done), kind=kOutput, calls=%fused_computation.15 | convolution fusion | flops 2148532224 | bytes 19136512 | tf_op jit(solution)/shard_map/dot_general | solution.py:178
  709.4 16.7 %all-to-all-done = bf16[16,64,2048]{2,1,0:T(8,128)(2,1)} async-done(((bf16[16,64,2048]{2,1,0:T(8,128)(2,1)}), bf16[16,64,2048]{2,1,0:T(8,128)(2,1)}, u32[]{:S(2)}, u32[]{:S(2)}) %all-to-all-start) | async-done | bytes 4194336 | tf_op jit(solution)/shard_map/all_to_all | solution.py:196
  726.1 6.5 copy.122
  732.6 5.0 all-to-all-start.1
  742.9 43.2 %all-to-all-done.1 = bf16[16,64,2048]{2,0,1:T(8,128)(2,1)} async-done(((bf16[16,64,2048]{2,0,1:T(8,128)(2,1)}), bf16[16,64,2048]{2,0,1:T(8,128)(2,1)}, u32[]{:S(2)}, u32[]{:S(2)}) %all-to-all-start.1) | async-done | bytes 4194336 | tf_op jit(solution)/shard_map/all_to_all | solution.py:195
  (137 shorter events, 70.2 us)
Async XLA Ops:
  7.2 113.7 %all-gather.9.cloned.1.call-start = ((), (), s32[]{:S(2)}) async-start(), calls=%async_computation.6 | async-start | bytes 10649600 | tf_op jit(solution)/shard_map/all_gather | solution.py:120
  32.9 183.4 %reduce-scatter.5.cloned.1.call-start = ((), (), s32[]{:S(2)}) async-start(), calls=%async_computation.7 | async-start | bytes 8912896 | tf_op jit(solution)/shard_map/reduce_scatter | solution.py:139
  131.6 84.7 %copy-start.9 = (bf16[128,2048]{1,0:T(8,128)(2,1)S(1)}, bf16[128,2048]{1,0:T(8,128)(2,1)}, u32[]{:S(2)}) copy-start(bf16[128,2048]{1,0:T(8,128)(2,1)} %param.22) | copy-start | bytes 1572868
  131.7 101.2 %copy-start.11 = (s32[1,3]{1,0:T(1,128)S(1)}, s32[1,3]{1,0:T(1,128)}, u32[]{:S(2)}) copy-start(s32[1,3]{1,0:T(1,128)} %param.23) | copy-start | bytes 40
  131.7 267.2 %copy-start.12 = (f32[1,8192]{1,0:T(1,128)S(1)}, f32[1,8192]{1,0:T(1,128)}, u32[]{:S(2)}) copy-start(f32[1,8192]{1,0:T(1,128)} %param.24) | copy-start | bytes 98308
  131.7 98.1 %all-gather.11.cloned.1.call-start = ((), (), s32[]{:S(2)}) async-start(), calls=%async_computation.8 | async-start | bytes 1572864 | tf_op jit(solution)/shard_map/all_gather | solution.py:160
  218.3 46.0 %all-gather.13.cloned.1.call-start = ((), (), s32[]{:S(2)}) async-start(), calls=%async_computation.9 | async-start | bytes 2621440 | tf_op jit(solution)/shard_map/all_gather | solution.py:174
  231.7 167.1 %all-gather.15.cloned.1.call-start = ((), (), s32[]{:S(2)}) async-start(), calls=%async_computation.10 | async-start | bytes 22282240 | tf_op jit(solution)/shard_map/all_gather | solution.py:149
  232.3 279.5 %all-gather.17.cloned.1.call-start = ((), (), s32[]{:S(2)}) async-start(), calls=%async_computation.11 | async-start | bytes 17825792 | tf_op jit(solution)/shard_map/all_gather | solution.py:150
  232.8 321.6 %reduce-scatter.7.cloned.1.call-start = ((), (), s32[]{:S(2)}) async-start(), calls=%async_computation.12 | async-start | bytes 2621440 | tf_op jit(solution)/shard_map/reduce_scatter | solution.py:181
  511.8 42.6 %copy-start.4 = (bf16[256,2048]{1,0:T(8,128)(2,1)S(1)}, bf16[256,2048]{1,0:T(8,128)(2,1)}, u32[]{:S(2)}) copy-start(bf16[256,2048]{1,0:T(8,128)(2,1)} %all-gather.11.cloned.1.call-done) | copy-start | bytes 3145732
  524.6 66.0 %all-gather.19.cloned.1.call-start = ((), (), s32[]{:S(2)}) async-start(), calls=%async_computation.13 | async-start | bytes 2621440 | tf_op jit(solution)/shard_map/all_gather | solution.py:174
  555.6 3.3 collective-permute-start
  559.8 87.1 %reduce-scatter.9.cloned.1.call-start = ((), (), s32[]{:S(2)}) async-start(), calls=%async_computation.14 | async-start | bytes 2621440 | tf_op jit(solution)/shard_map/reduce_scatter | solution.py:181
  559.9 3.1 collective-permute-start.1
  604.1 42.7 %copy-start.2 = (bf16[128,2048]{1,0:T(8,128)(2,1)S(1)}, bf16[128,2048]{1,0:T(8,128)(2,1)}, u32[]{:S(2)}) copy-start(bf16[128,2048]{1,0:T(8,128)(2,1)} %slice_select_fusion.1) | copy-start | bytes 1572868
  617.0 66.1 %all-gather.21.cloned.1.call-start = ((), (), s32[]{:S(2)}) async-start(), calls=%async_computation.15 | async-start | bytes 2621440 | tf_op jit(solution)/shard_map/all_gather | solution.py:174
  648.1 3.3 collective-permute-start.2
  655.3 70.8 %all-to-all-start = ((bf16[16,64,2048]{2,1,0:T(8,128)(2,1)}), bf16[16,64,2048]{2,1,0:T(8,128)(2,1)}, u32[]{:S(2)}, u32[]{:S(2)}) async-start(bf16[16,64,2048]{2,1,0:T(8,128)(2,1)} %bitcast.188), calls=%async_computation.4 | async-start | bytes 8388608 | tf_op jit(solution)/shard_map/all_to_all | solution.py:196
  662.2 77.1 %reduce-scatter.11.cloned.1.call-start = ((), (), s32[]{:S(2)}) async-start(), calls=%async_computation.16 | async-start | bytes 2621440 | tf_op jit(solution)/shard_map/reduce_scatter | solution.py:181
  662.2 2.8 collective-permute-start.3
  732.6 53.5 %all-to-all-start.1 = ((bf16[16,64,2048]{2,0,1:T(8,128)(2,1)}), bf16[16,64,2048]{2,0,1:T(8,128)(2,1)}, u32[]{:S(2)}, u32[]{:S(2)}) async-start(bf16[16,64,2048]{2,0,1:T(8,128)(2,1)} %copy.122), calls=%async_computation.5 | async-start | bytes 8388608 | tf_op jit(solution)/shard_map/all_to_all | solution.py:195
  737.6 53.2 %all-reduce.3.cloned.1.call-start = ((), (), s32[]{:S(2)}) async-start(), calls=%async_computation.17 | async-start | bytes 2097152 | tf_op jit(solution)/shard_map/psum | solution.py:28
  740.5 52.1 %copy-start.1 = (bf16[1280,1280]{1,0:T(8,128)(2,1)S(1)}, bf16[1280,1280]{1,0:T(8,128)(2,1)}, u32[]{:S(2)}) copy-start(bf16[1280,1280]{1,0:T(8,128)(2,1)} %param.18) | copy-start | bytes 9830404
  (11 other events, 127.5 us)
Sparse Core Ops, SparseCore 0:
  33.0 87.8 all-gather.8
  131.8 84.5 reduce-scatter.4
  218.6 11.1 all-gather.10
  231.9 32.4 all-gather.12
  266.3 132.4 all-gather.14
  400.8 110.9 all-gather.16
  524.8 29.5 reduce-scatter.6
  559.9 30.6 all-gather.18
  617.1 29.7 reduce-scatter.8
  652.3 30.6 all-gather.20
  709.5 29.7 reduce-scatter.10
  743.0 26.6 all-reduce.2
where the time goes:
time: 808 us; the launch traced here: 800 us
  waiting for transfers between devices  590 us (73%)
  matrix products  97.5 us (12%)
  other arithmetic  27.1 us (3%)
  blocking collectives  26.8 us (3%)
  local copies, waits for them, and re-layouts  21.7 us (3%)
  starting transfers between devices  20.8 us (3%)
  between operations  15.7 us (2%)
    all_gather x1, waiting for transfers between devices, shards(): lax.all_gather(w_qkv, 'dp', axis=1, tiled=True)  132 us
    all_gather x1, waiting for transfers between devices, shards(): lax.all_gather(wo_t, 'dp', axis=1, tiled=True)  102 us
    reduce_scatter x1, waiting for transfers between devices, shards(): lax.psum_scatter(jnp.dot(picked, w_merge, preferred_element_type=jnp.floa...  83.9 us
    all_gather x3, waiting for transfers between devices, shards(): features = lax.all_gather(carried, 'mp', axis=1, tiled=True)  74.1 us
    reduce_scatter x3, waiting for transfers between devices, shards(): lax.psum_scatter(partial_value.astype(jnp.bfloat16), 'mp', scatter_dimens...  61.3 us
    all_gather x1, waiting for transfers between devices, shards(): lax.all_gather(merged, ('dp', 'mp'), axis=0, tiled=True)  60.5 us
    all_to_all x1, waiting for transfers between devices, shards(): lax.all_to_all(lax.all_to_all(outgoing, 'dp', split_axis=0, concat_axis=0...  43.2 us
    dot_general x3, matrix products, shards(): lax.dot_general(attended, out_weight, (((1,), (1,)), ((), ())), preferred...  38.4 us
  transfers between devices with their start and end apart: 18, of which 17 were waited for; matrix products, arithmetic and copies ran while one was open for 8% of the time, Pallas kernels for 0%

commit v1 on v0

v1 whole, which is shorter than its diff:
```python
import functools
import math

import jax
import jax.numpy as jnp
from jax import lax
from jax.experimental import pallas as pl
from jax.experimental.pallas import tpu as pltpu
from jax.sharding import PartitionSpec as P

QH = 32
KVH = 4
HD = 128
VD = 1280
VH = 16
VHD = 80
MERGE = 4
SIDE = 4
TOK = 128
FB = 512
HEADS = QH // KVH
QW = HEADS * HD
PW = QW + 2 * HD
PT = PW + HD
D = 8192
EPSILON = 1e-06
VMEM_LIMIT = 56 * 1024 * 1024
BF = jnp.bfloat16
F32 = jnp.float32


def layer_norm(values, norm_gain):
    values = values.astype(F32)
    centre = jnp.mean(values, axis=-1, keepdims=True)
    centred = values - centre
    variance = jnp.mean(centred * centred, axis=-1, keepdims=True)
    return centred * lax.rsqrt(variance + EPSILON) * norm_gain


def segment_of(lengths, amount):
    boundary = jnp.cumsum(lengths.astype(jnp.int32))
    positions = jnp.arange(amount, dtype=jnp.int32)
    return jnp.sum((positions[:, None] >= boundary[None, :]).astype(jnp.int32), axis=1)


def vision_rows(patches, units, v_gain, v_qkv, v_out, merge_gain):
    amount = patches.shape[0]
    merged_count = amount // MERGE
    unit_image = segment_of(units, merged_count)
    image_ids = jnp.broadcast_to(unit_image[:, None], (merged_count, MERGE)).reshape(amount)
    v_normed = layer_norm(patches, v_gain).astype(BF)
    projected = jnp.dot(v_normed, v_qkv, preferred_element_type=F32).astype(BF)
    projected = projected.reshape(amount, 3, VH, VHD)
    scores = jnp.einsum(
        "qhd,khd->hqk", projected[:, 0], projected[:, 1], preferred_element_type=F32
    ) / math.sqrt(VHD)
    allowed = image_ids[:, None] == image_ids[None, :]
    scores = jnp.where(allowed[None], scores, -1e30)
    weights = jax.nn.softmax(scores, axis=-1).astype(BF)
    attended = (
        jnp.einsum("hqk,khd->qhd", weights, projected[:, 2], preferred_element_type=F32)
        .astype(BF)
        .reshape(amount, VD)
    )
    update = jnp.dot(attended, v_out, preferred_element_type=F32)
    v_hidden = (patches.astype(F32) + update).astype(BF)
    merged = layer_norm(v_hidden, merge_gain).astype(BF)
    return merged.reshape(merged_count, MERGE * VD)


def push(src, dst, send_sem, recv_sem, where):
    copy = pltpu.make_async_remote_copy(
        src_ref=src,
        dst_ref=dst,
        send_sem=send_sem,
        recv_sem=recv_sem,
        device_id=where,
        device_id_type=pl.DeviceIdType.MESH,
    )
    copy.start()
    return copy


def greet(partners):
    barrier = pltpu.get_barrier_semaphore()
    for where in partners:
        pl.semaphore_signal(
            barrier, inc=1, device_id=where, device_id_type=pl.DeviceIdType.MESH
        )
    pl.semaphore_wait(barrier, len(partners))


def along(index, step):
    return lax.rem(index + step, SIDE)


def behind(index, step):
    return lax.rem(index + SIDE - step, SIDE)


def merge_kernel(
    pieces, wm, text, lslot, gslot, grads,
    h0, mg,
    wmv, xbuf, part, psend, rbuf, ybuf, tbuf, pick, gbuf, gsend, grec, gz, mz,
    w_sem, s_pl, r_pl, s_x, r_x, s_y, r_y, s_t, r_t, s_g, r_g, s_gy, r_gy, s_gz, r_gz,
):
    x = lax.axis_index("x")
    y = lax.axis_index("y")
    z = lax.axis_index("mp")
    plane = [(dx, dz) for dx in range(SIDE) for dz in range(SIDE) if dx or dz]
    steps = (1, 3, 2)

    loads = []
    for dx in range(SIDE):
        xt = along(x, dx)
        load = pltpu.make_async_copy(
            wm.at[:, pl.ds(pl.multiple_of(xt * FB, FB), FB)], wmv.at[dx], w_sem.at[dx]
        )
        load.start()
        loads.append(load)

    greet(
        [{"x": along(x, dx), "mp": along(z, dz)} for dx, dz in plane]
        + [{"y": along(y, dy)} for dy in steps]
    )
    plane_copies = []
    for dx, dz in plane:
        xt = along(x, dx)
        plane_copies.append(
            push(
                pieces.at[xt], xbuf.at[x * SIDE + z],
                s_pl.at[dx * SIDE + dz], r_pl.at[dx * SIDE + dz],
                {"x": xt, "mp": along(z, dz)},
            )
        )
    xbuf[x * SIDE + z] = pieces[x]
    text_copies, grad_copies = [], []
    for dx in steps:
        xt = along(x, dx)
        text_copies.append(
            push(
                text.at[:, pl.ds(pl.multiple_of(xt * FB, FB), FB)], tbuf.at[x],
                s_t.at[dx], r_t.at[dx], {"x": xt},
            )
        )
    tbuf[x] = text[:, pl.ds(pl.multiple_of(x * FB, FB), FB)]
    for dx in steps:
        grad_copies.append(
            push(grads, gbuf.at[x], s_g.at[dx], r_g.at[dx], {"x": along(x, dx)})
        )
    gbuf[x] = grads[...]

    slots = lslot[...]
    for block in range(SIDE):
        wanted = lax.broadcasted_iota(jnp.int32, (TOK, slots.shape[1]), 0) + block * TOK
        pick[pl.ds(block * TOK, TOK), :] = jnp.where(wanted == slots, 1.0, 0.0).astype(BF)

    for load in loads:
        load.wait()
    for copy in plane_copies:
        copy.wait()

    rows = xbuf[...].reshape(SIDE * SIDE * 16, VD)
    x_copies = []
    for dx in steps:
        psend[dx] = jnp.dot(rows, wmv[dx], preferred_element_type=F32).astype(BF)
        x_copies.append(
            push(psend.at[dx], rbuf.at[dx], s_x.at[dx], r_x.at[dx], {"x": along(x, dx)})
        )
    part[...] = jnp.dot(rows, wmv[0], preferred_element_type=F32)
    for copy in x_copies:
        copy.wait()
    total = part[...]
    for dx in steps:
        total = total + rbuf[dx].astype(F32)
    ybuf[y] = total.astype(BF)
    y_copies = [
        push(ybuf.at[y], ybuf.at[y], s_y.at[dy], r_y.at[dy], {"y": along(y, dy)})
        for dy in steps
    ]

    for copy in grad_copies:
        copy.wait()
    given = gbuf[...].reshape(SIDE * TOK, grads.shape[1])
    gy_copies = []
    for dy in (1, 3, 2, 0):
        yt = along(y, dy)
        mine = gslot[pl.ds(pl.multiple_of(yt * 64, 64), 64), :]
        lanes = lax.broadcasted_iota(jnp.int32, (64, SIDE * TOK), 1)
        chosen = jnp.where(lanes == mine, 1.0, 0.0).astype(BF)
        gsend[dy] = jnp.dot(chosen, given, preferred_element_type=F32).astype(BF)
        if dy:
            gy_copies.append(
                push(gsend.at[dy], grec.at[dy], s_gy.at[dy], r_gy.at[dy], {"y": yt})
            )

    for copy in text_copies:
        copy.wait()
    for copy in y_copies:
        copy.wait()
    chosen = pick[...]
    picked = jnp.dot(
        chosen, ybuf[...].reshape(SIDE * 256, FB), preferred_element_type=F32
    ).astype(BF)
    present = jnp.dot(chosen, jnp.ones((SIDE * 256, 128), BF), preferred_element_type=F32)
    texts = tbuf[...].reshape(SIDE * TOK, FB)
    for tile in range(FB // 128):
        cols = slice(tile * 128, (tile + 1) * 128)
        h0[:, cols] = jnp.where(present > 0.5, picked[:, cols], texts[:, cols])

    for copy in gy_copies:
        copy.wait()
    found = gsend[0].astype(F32)
    for dy in steps:
        found = found + grec[dy].astype(F32)
    gz[...] = found.astype(BF).reshape(SIDE, 16, grads.shape[1])
    gz_copies = []
    for dz in steps:
        zt = along(z, dz)
        gz_copies.append(push(gz.at[zt], mz.at[z], s_gz.at[dz], r_gz.at[dz], {"mp": zt}))
    mz[z] = gz[z]
    for copy in gz_copies:
        copy.wait()
    width = grads.shape[1]
    for block in range(SIDE):
        mg[:, block * width : (block + 1) * width] = mz[block]


def merge_call(pieces, wm, text, lslot, gslot, grads):
    vmem = pl.BlockSpec(memory_space=pltpu.VMEM)
    dma = pltpu.SemaphoreType.DMA
    width = grads.shape[1]
    return pl.pallas_call(
        merge_kernel,
        out_shape=(
            jax.ShapeDtypeStruct((SIDE * TOK, FB), BF),
            jax.ShapeDtypeStruct((16, SIDE * width), BF),
        ),
        in_specs=[vmem, pl.BlockSpec(memory_space=pl.ANY), vmem, vmem, vmem, vmem],
        out_specs=(vmem, vmem),
        scratch_shapes=[
            pltpu.VMEM((SIDE, VD, FB), BF),
            pltpu.VMEM((SIDE * SIDE, 16, VD), BF),
            pltpu.VMEM((256, FB), F32),
            pltpu.VMEM((SIDE, 256, FB), BF),
            pltpu.VMEM((SIDE, 256, FB), BF),
            pltpu.VMEM((SIDE, 256, FB), BF),
            pltpu.VMEM((SIDE, TOK, FB), BF),
            pltpu.VMEM((SIDE * TOK, 1024), BF),
            pltpu.VMEM((SIDE, TOK, width), BF),
            pltpu.VMEM((SIDE, 64, width), BF),
            pltpu.VMEM((SIDE, 64, width), BF),
            pltpu.VMEM((SIDE, 16, width), BF),
            pltpu.VMEM((SIDE, 16, width), BF),
            dma((SIDE,)),
            dma((16,)), dma((16,)),
            dma((SIDE,)), dma((SIDE,)),
            dma((SIDE,)), dma((SIDE,)),
            dma((SIDE,)), dma((SIDE,)),
            dma((SIDE,)), dma((SIDE,)),
            dma((SIDE,)), dma((SIDE,)),
            dma((SIDE,)), dma((SIDE,)),
        ],
        compiler_params=pltpu.CompilerParams(
            collective_id=1, has_side_effects=True, vmem_limit_bytes=VMEM_LIMIT
        ),
        name="merge",
    )(pieces, wm, text, lslot, gslot, grads)


def layer_kernel(
    layer, last,
    h, wqa, wqb, woa, wob, mask,
    out,
    wq, wo, zbuf, acc, squares, psend, rbuf, abuf, osend, orec, obuf,
    w_sem, s_z, r_z, s_x, r_x, s_a, r_a, s_o, r_o, s_e, r_e,
):
    x = lax.axis_index("x")
    z = lax.axis_index("mp")
    section = lax.axis_index("section")
    steps = (1, 3, 2)

    @pl.when(section == layer)
    def _():
        pltpu.make_async_copy(wqa, wq, w_sem.at[0]).start()
        pltpu.make_async_copy(woa, wo, w_sem.at[1]).start()

    @pl.when(section != layer)
    def _():
        pltpu.make_async_copy(wqb, wq, w_sem.at[0]).start()
        pltpu.make_async_copy(wob, wo, w_sem.at[1]).start()

    zbuf[z] = h[...]
    greet([{"x": along(x, d)} for d in steps] + [{"mp": along(z, d)} for d in steps])
    z_copies = {
        dz: push(zbuf.at[z], zbuf.at[z], s_z.at[dz], r_z.at[dz], {"mp": along(z, dz)})
        for dz in steps
    }
    pltpu.make_async_copy(wqa, wq, w_sem.at[0]).wait()
    for dz in (0, 1, 3, 2):
        zs = behind(z, dz)
        if dz:
            z_copies[dz].wait_recv()
        block = zbuf[zs]
        wide = block.astype(F32)
        wide = wide * wide
        squared = jnp.sum(wide, axis=1, keepdims=True)
        if dz:
            squares[...] += jnp.broadcast_to(squared, squares.shape)
        else:
            squares[...] = jnp.broadcast_to(squared, squares.shape)

        @pl.loop(0, PW // 256)
        def _(tile):
            cols = pl.ds(pl.multiple_of(tile * 256, 256), 256)
            product = jnp.dot(zbuf[zs], wq[zs, :, cols], preferred_element_type=F32)
            if dz:
                acc[:, cols] += product
            else:
                acc[:, cols] = product

    lane = lax.broadcasted_iota(jnp.int32, (TOK, HD), 1)
    x_copies = []
    for dx in steps:
        xt = along(x, dx)
        span = pl.ds(pl.multiple_of(xt * TOK, TOK), TOK)
        psend[dx, :, :PW] = acc[span, :].astype(BF)
        sq = squares[span, :]
        high = sq.astype(BF)
        low = (sq - high.astype(F32)).astype(BF)
        psend[dx, :, PW:] = jnp.where(lane < 64, high, low)
        x_copies.append(
            push(psend.at[dx], rbuf.at[dx], s_x.at[dx], r_x.at[dx], {"x": xt})
        )
    own = pl.ds(pl.multiple_of(x * TOK, TOK), TOK)
    total = acc[own, :]
    sq = squares[own, :][:, :1]
    for copy in x_copies:
        copy.wait()
    for dx in steps:
        total = total + rbuf[dx, :, :PW].astype(F32)
        tail = rbuf[dx, :, PW:].astype(F32)
        sq = sq + tail[:, :1] + tail[:, 64:65]
    scale = lax.rsqrt(sq / D + EPSILON)
    projected = (total * scale).astype(BF)
    keys = projected[:, QW : QW + HD]
    values = projected[:, QW + HD :]
    allowed = mask[...] > 0.5
    for head in range(HEADS):
        cols = slice(head * HD, (head + 1) * HD)
        scores = lax.dot_general(
            projected[:, cols], keys, (((1,), (1,)), ((), ())), preferred_element_type=F32
        ) * (1.0 / math.sqrt(HD))
        scores = jnp.where(allowed, scores, -1e30)
        top = jnp.max(scores, axis=1, keepdims=True)
        weights = jnp.exp(scores - top)
        weights = (weights / jnp.sum(weights, axis=1, keepdims=True)).astype(BF)
        abuf[x, :, cols] = jnp.dot(weights, values, preferred_element_type=F32).astype(BF)
    a_copies = [
        push(abuf.at[x], abuf.at[x], s_a.at[dx], r_a.at[dx], {"x": along(x, dx)})
        for dx in steps
    ]
    pltpu.make_async_copy(woa, wo, w_sem.at[1]).wait()
    for copy in a_copies:
        copy.wait()
    o_copies = []
    for dz in (1, 3, 2, 0):
        zt = along(z, dz)

        @pl.loop(0, FB // 256)
        def _(tile):
            cols = pl.ds(pl.multiple_of(tile * 256, 256), 256)
            osend[dz, :, cols] = lax.dot_general(
                abuf[...].reshape(SIDE * TOK, QW), wo[zt, cols, :],
                (((1,), (1,)), ((), ())), preferred_element_type=F32,
            ).astype(BF)

        if dz:
            o_copies.append(
                push(osend.at[dz], orec.at[dz], s_o.at[dz], r_o.at[dz], {"mp": zt})
            )
    for copy in z_copies.values():
        copy.wait_send()
    update = osend[0].astype(F32)
    for copy in o_copies:
        copy.wait()
    for dz in steps:
        update = update + orec[dz].astype(F32)
    fresh = (h[...].astype(F32) + update).astype(BF)
    if not last:
        out[...] = fresh
        return
    zbuf[0] = fresh
    e_copies = []
    for dx in steps:
        xt = along(x, dx)
        e_copies.append(
            push(
                zbuf.at[0, pl.ds(pl.multiple_of(xt * TOK, TOK), TOK), :], obuf.at[x],
                s_e.at[dx], r_e.at[dx], {"x": xt},
            )
        )
    obuf[x] = zbuf[0, own, :]
    for copy in e_copies:
        copy.wait()
    for block in range(SIDE):
        out[:, block * FB : (block + 1) * FB] = obuf[block]


def layer_call(layer, last, h, wqa, wqb, woa, wob, mask):
    vmem = pl.BlockSpec(memory_space=pltpu.VMEM)
    hbm = pl.BlockSpec(memory_space=pl.ANY)
    dma = pltpu.SemaphoreType.DMA
    rows = SIDE * TOK
    return pl.pallas_call(
        functools.partial(layer_kernel, layer, last),
        out_shape=jax.ShapeDtypeStruct((TOK, SIDE * FB) if last else (rows, FB), BF),
        in_specs=[vmem, hbm, hbm, hbm, hbm, vmem],
        out_specs=vmem,
        scratch_shapes=[
            pltpu.VMEM((SIDE, FB, PW), BF),
            pltpu.VMEM((SIDE, FB, QW), BF),
            pltpu.VMEM((SIDE, rows, FB), BF),
            pltpu.VMEM((rows, PW), F32),
            pltpu.VMEM((rows, HD), F32),
            pltpu.VMEM((SIDE, TOK, PT), BF),
            pltpu.VMEM((SIDE, TOK, PT), BF),
            pltpu.VMEM((SIDE, TOK, QW), BF),
            pltpu.VMEM((SIDE, rows, FB), BF),
            pltpu.VMEM((SIDE, rows, FB), BF),
            pltpu.VMEM((SIDE, TOK, FB), BF),
            dma((2,)),
            dma((SIDE,)), dma((SIDE,)),
            dma((SIDE,)), dma((SIDE,)),
            dma((SIDE,)), dma((SIDE,)),
            dma((SIDE,)), dma((SIDE,)),
            dma((SIDE,)), dma((SIDE,)),
        ],
        compiler_params=pltpu.CompilerParams(
            collective_id=2 + layer, has_side_effects=True, vmem_limit_bytes=VMEM_LIMIT
        ),
        name="layer%d" % layer,
    )(h, wqa, wqb, woa, wob, mask)


def shards(
    patches,
    image_units,
    v_gain,
    v_qkv,
    v_out,
    merge_gain,
    w_merge,
    routes,
    text,
    seq_lengths,
    lang_gain,
    w_qkv,
    wo_t,
    row_grads,
):
    x = lax.axis_index("x")
    y = lax.axis_index("y")
    swap = [(0, 1), (1, 0)]

    wm = lax.all_gather(w_merge, "y", axis=0, tiled=True)
    gain = lax.dynamic_slice_in_dim(lang_gain[0], (y * SIDE + x) * FB, FB, 0)
    scaled = (w_qkv[0].astype(F32) * gain[:, None]).astype(BF)
    wq_here = lax.all_gather(scaled, "y", axis=0, tiled=False)
    wo_here = lax.all_gather(wo_t[0], "y", axis=0, tiled=False)
    wq_there = lax.ppermute(wq_here, "section", swap)
    wo_there = lax.ppermute(wo_here, "section", swap)

    target = lax.all_gather(routes, ("y", "x", "mp"), axis=0, tiled=True)[:, 0]
    count = target.shape[0]
    order = jnp.arange(count, dtype=jnp.int32)
    position = jnp.sum(
        ((target[:, None] == target[None, :]) & (order[:, None] > order[None, :])).astype(jnp.int32),
        axis=1,
    )
    local = (target - y * SIDE) * TOK + position
    gslot = lax.dynamic_index_in_dim(local.reshape(SIDE, SIDE, 64), x, 1, keepdims=False)

    merged = vision_rows(patches, image_units[0], v_gain, v_qkv, v_out, merge_gain)
    pieces = merged.reshape(16, MERGE, SIDE, 320).transpose(2, 0, 1, 3).reshape(SIDE, 16, VD)

    hidden, merged_grads = merge_call(
        pieces, wm, text, local[None, :], gslot.reshape(256, 1), row_grads
    )
    seq = segment_of(seq_lengths[0], TOK)
    at = jnp.arange(TOK, dtype=jnp.int32)
    mask = ((seq[:, None] == seq[None, :]) & (at[:, None] >= at[None, :])).astype(F32)
    hidden = layer_call(0, False, hidden, wq_here, wq_there, wo_here, wo_there, mask)
    final_hidden = layer_call(1, True, hidden, wq_here, wq_there, wo_here, wo_there, mask)
    return (final_hidden, merged_grads)


def solution(mesh):
    grid = jax.sharding.Mesh(
        mesh.devices.reshape(2, SIDE, SIDE, SIDE), ("section", "y", "x", "mp")
    )
    every = ("section", "y", "x", "mp")
    home = P(("section", "y", "x"), "mp")
    in_specs = (
        P(every, None),
        P(every, None),
        P(),
        P(),
        P(),
        P(),
        P(("y", "x"), "mp"),
        P(every, None),
        home,
        P(("section", "y", "x"), None),
        P("section", None),
        P("section", ("y", "x"), "mp"),
        P("section", ("y", "x"), "mp"),
        home,
    )
    out_specs = (home, P(every, None))
    return jax.shard_map(shards, mesh=grid, in_specs=in_specs, out_specs=out_specs, check_vma=False)
```

time: 808 us -> 430 us (0.53)
  waiting for transfers between devices: 590 us -> 116 us
  Pallas kernels: 0 us -> 240 us
  matrix products: 97.5 us -> 10.9 us
  other arithmetic: 27.1 us -> 5.53 us
  starting transfers between devices: 20.8 us -> 0.12 us
    all_gather x7 -> x3, waiting for transfers between devices: 380 us -> 115 us  [the longest x1 58.1 us: shards(): wq_here = lax.all_gather(scaled, 'y', axis=0, tiled=False)]
    pallas_call x0 -> x3, Pallas kernels: none -> 240 us  [the longest x2 155 us: layer_call(): pl.pallas_call(functools.partial(layer_kernel, layer, last), out_shape=ja...]
    reduce_scatter x4 -> x0, waiting for transfers between devices: 145 us -> none  [the longest x1 83.9 us: shards(): lax.psum_scatter(jnp.dot(picked, w_merge, preferred_element_type=jnp.floa...]
    dot_general x16 -> x2, matrix products: 93.8 us -> 8.19 us  [the longest x1 6.47 us: vision_rows(): projected = jnp.dot(v_normed, v_qkv, preferred_element_type=F32).astype(BF)]
    all_to_all x2 -> x0, waiting for transfers between devices: 59.9 us -> none  [the longest x1 43.2 us: shards(): lax.all_to_all(lax.all_to_all(outgoing, 'dp', split_axis=0, concat_axis=0...]
    squeeze x1 -> x0, blocking collectives: 24.9 us -> none  [shards(): target = all_routes[:, 0]]
    eq x0 -> x1, blocking collectives: none -> 22.4 us  [shards(): target[:, None] == target[None, :]]
    all_to_all x2 -> x0, starting transfers between devices: 11.9 us -> none  [the longest x1 6.88 us: shards(): lax.all_to_all(outgoing, 'dp', split_axis=0, concat_axis=0, tiled=True)]
  transfers between devices with their start and end apart: 18 -> 5, of which waited for: 17 -> 3; matrix products, arithmetic and copies ran while one was open for 8% -> 7% of each run, Pallas kernels for 0% -> 20%
where the time goes in v1:
time: 430 us; the launch traced here: 429 us
  Pallas kernels  240 us (56%)
  waiting for transfers between devices  116 us (27%)
  blocking collectives  22.4 us (5%)
  local copies, waits for them, and re-layouts  19.3 us (4%)
  between operations  14.6 us (3%)
  matrix products  10.9 us (3%)
  other arithmetic  5.53 us (1%)
    pallas_call x2, Pallas kernels, layer_call(): pl.pallas_call(functools.partial(layer_kernel, layer, last), out_shape=ja...  155 us
    pallas_call x1, Pallas kernels, merge_call(): pl.pallas_call(merge_kernel, out_shape=(jax.ShapeDtypeStruct((SIDE * TOK,...  85.5 us
    all_gather x1, waiting for transfers between devices, shards(): wq_here = lax.all_gather(scaled, 'y', axis=0, tiled=False)  58.1 us
    all_gather x1, waiting for transfers between devices, shards(): wm = lax.all_gather(w_merge, 'y', axis=0, tiled=True)  31.1 us
    all_gather x1, waiting for transfers between devices, shards(): wo_here = lax.all_gather(wo_t[0], 'y', axis=0, tiled=False)  25.8 us
    eq x1, blocking collectives, shards(): target[:, None] == target[None, :]  22.4 us
  transfers between devices with their start and end apart: 5, of which 3 were waited for; matrix products, arithmetic and copies ran while one was open for 7% of the time, Pallas kernels for 20%

profile of v1, /device:TPU:0, one launch (start us, length us, event | category | flops | bytes accessed | tf_op | source)
XLA Modules:
  0.0 429.5 jit_solution(15193870120202122541)
XLA Ops:
  7.3 0.8 constant_dynamic-slice_fusion
  8.1 2.9 multiply_convert_fusion
  12.5 58.1 %all-gather.6.cloned.1.call-done.wqa = bf16[4,512,1280]{2,1,0:T(8,128)(2,1)} async-done(((bf16[1,512,1280]{2,1,0:T(8,128)(2,1)}), bf16[4,512,1280]{2,1,0:T(8,128)(2,1)}) %all-gather.6.cloned.1.call-update) | async-done | bytes 5242896 | tf_op jit(solution)/shard_map/all_gather | solution.py:469
  72.4 22.4 %all-reduce = s32[1024]{0:T(1024)S(1)} all-reduce(s32[1024]{0:T(1024)S(1)} %bitcast_dynamic-update-slice_fusion), channel_id=1, replica_groups=mesh['section'=2,'y'=4,'x'=4,'mp'=4] {'y','x','mp'}, use_global_device_ids=true, to_apply=%add | all-reduce | flops 1024 | bytes 8192 | tf_op jit(solution)/shard_map/eq | solution.py:478
  95.4 25.8 %all-gather.8.cloned.1.call-done.woa = bf16[4,512,1024]{2,1,0:T(8,128)(2,1)} async-done(((bf16[1,512,1024]{2,1,0:T(8,128)(2,1)}), bf16[4,512,1024]{2,1,0:T(8,128)(2,1)}) %all-gather.8.cloned.1.call-update) | async-done | bytes 4194320 | tf_op jit(solution)/shard_map/all_gather | solution.py:470
  121.5 0.8 reshape.192.gslot
  122.7 6.5 %convolution_convert_fusion = bf16[64,3840]{1,0:T(8,128)(2,1)} fusion(bf16[1280,3840]{1,0:T(8,128)(2,1)} %param.17, bf16[64,1280]{1,0:T(8,128)(2,1)S(1)} %copy-done.1, f32[1280]{0:T(1024)S(1)} %copy-done.4, f32[64]{0:T(128)S(1)} %add_rsqrt_fusion.1, f32[64]{0:T(128)S(1)} %broadcast_multiply_fusion.1), kind=kOutput, calls=%fused_computation.1 | convolution fusion | flops 629800960 | bytes 10491392 | tf_op jit(solution)/shard_map/dot_general | solution.py:52
  129.2 3.0 reshape.170
  132.3 2.1 fusion.21
  134.6 0.8 copy-done.9
  135.6 2.4 fusion.7
  138.0 1.8 copy.39
  139.8 1.9 reshape.173
  141.7 1.7 fusion.23
  143.8 0.9 reshape_reshape.3
  144.7 1.7 copy.53
  146.4 1.8 reshape.174.pieces
  148.3 0.7 fusion.19.mask
  149.0 31.1 %all-gather.4.cloned.1.call-done.wm = bf16[1280,2048]{1,0:T(8,128)(2,1)} async-done(((bf16[320,2048]{1,0:T(8,128)(2,1)}), bf16[1280,2048]{1,0:T(8,128)(2,1)}) %all-gather.4.cloned.1.call-update) | async-done | bytes 5242896 | tf_op jit(solution)/shard_map/all_gather | solution.py:466
  180.2 85.5 %merge.1 = (bf16[512,512]{1,0:T(8,128)(2,1)}, bf16[16,8192]{1,0:T(8,128)(2,1)}) custom-call(bf16[4,16,1280]{2,1,0:T(8,128)(2,1)} %reshape.174.pieces, bf16[1280,2048]{1,0:T(8,128)(2,1)} %all-gather.4.cloned.1.call-done.wm, bf16[128,2048]{1,0:T(8,128)(2,1)} %text.1, s32[1,1024]{1,0:T(1,128)} %bitcast.29, s32[256,1]{1,0:T(8,128)} %reshape.192.gslot, ...), custom_call_target="tpu_custom_call" | custom-call | tf_op jit(solution)/shard_map/merge/pallas_call | solution.py:233
  265.7 76.7 %layer0.1.h = bf16[512,512]{1,0:T(8,128)(2,1)} custom-call(bf16[512,512]{1,0:T(8,128)(2,1)} %get-tuple-element.4.h, bf16[4,512,1280]{2,1,0:T(8,128)(2,1)} %all-gather.6.cloned.1.call-done.wqa, bf16[4,512,1280]{2,1,0:T(8,128)(2,1)} %collective-permute-done.wqb, bf16[4,512,1024]{2,1,0:T(8,128)(2,1)} %all-gather.8.cloned.1.call-done.woa, ...), custom_call_target="tpu_custom_call" | custom-call | tf_op jit(solution)/shard_map/layer0/pallas_call | solution.py:415
  342.4 78.0 %layer1.1 = bf16[128,2048]{1,0:T(8,128)(2,1)} custom-call(bf16[512,512]{1,0:T(8,128)(2,1)} %layer0.1.h, bf16[4,512,1280]{2,1,0:T(8,128)(2,1)} %all-gather.6.cloned.1.call-done.wqa, bf16[4,512,1280]{2,1,0:T(8,128)(2,1)} %collective-permute-done.wqb, bf16[4,512,1024]{2,1,0:T(8,128)(2,1)} %all-gather.8.cloned.1.call-done.woa, ...), custom_call_target="tpu_custom_call" | custom-call | tf_op jit(solution)/shard_map/layer1/pallas_call | solution.py:415
  420.4 1.9 copy.57
  422.2 0.7 copy.58
  (55 shorter events, 4.8 us)
Async XLA Ops:
  7.2 134.6 %copy-start = (bf16[1280,1280]{1,0:T(8,128)(2,1)S(1)}, bf16[1280,1280]{1,0:T(8,128)(2,1)}, u32[]{:S(2)}) copy-start(bf16[1280,1280]{1,0:T(8,128)(2,1)} %param.18) | copy-start | bytes 9830404
  7.2 63.8 %copy-start.10 = (u32[128]{0:T(128)S(1)}, u32[128]{0:T(128)}, u32[]{:S(2)}) copy-start(u32[128]{0:T(128)} %constant.55) | copy-start | bytes 1540
  7.2 63.5 %copy-start.6 = (s32[1,3]{1,0:T(1,128)S(1)}, s32[1,3]{1,0:T(1,128)}, u32[]{:S(2)}) copy-start(s32[1,3]{1,0:T(1,128)} %param.15) | copy-start | bytes 40
  7.2 63.6 %copy-start.7 = (s32[1,3]{1,0:T(1,128)S(1)}, s32[1,3]{1,0:T(1,128)}, u32[]{:S(2)}) copy-start(s32[1,3]{1,0:T(1,128)} %param.23) | copy-start | bytes 40
  7.2 65.0 %copy-start.8 = (s32[16,1]{0,1:T(1,128)S(1)}, s32[16,1]{0,1:T(1,128)}, u32[]{:S(2)}) copy-start(s32[16,1]{0,1:T(1,128)} %param.21) | copy-start | bytes 196
  7.2 115.1 %copy-start.1 = (bf16[64,1280]{1,0:T(8,128)(2,1)S(1)}, bf16[64,1280]{1,0:T(8,128)(2,1)}, u32[]{:S(2)}) copy-start(bf16[64,1280]{1,0:T(8,128)(2,1)} %param.14) | copy-start | bytes 491524
  7.2 115.5 %copy-start.4 = (f32[1280]{0:T(1024)S(1)}, f32[1280]{0:T(1024)}, u32[]{:S(2)}) copy-start(f32[1280]{0:T(1024)} %param.16) | copy-start | bytes 15364
  7.2 63.4 %all-gather.6.cloned.1.call-start = ((), (), s32[]{:S(2)}) async-start(), calls=%async_computation.1 | async-start | bytes 6553600 | tf_op jit(solution)/shard_map/all_gather | solution.py:469
  11.0 110.2 %all-gather.8.cloned.1.call-start = ((), (), s32[]{:S(2)}) async-start(), calls=%async_computation.2 | async-start | bytes 5242880 | tf_op jit(solution)/shard_map/all_gather | solution.py:470
  11.8 168.4 %all-gather.4.cloned.1.call-start = ((), (), s32[]{:S(2)}) async-start(), calls=%async_computation | async-start | bytes 6553600 | tf_op jit(solution)/shard_map/all_gather | solution.py:466
  70.6 195.0 %collective-permute-start = (bf16[4,512,1280]{2,1,0:T(8,128)(2,1)}, bf16[4,512,1280]{2,1,0:T(8,128)(2,1)}, u32[]{:S(2)}, u32[]{:S(2)}) collective-permute-start(bf16[4,512,1280]{2,1,0:T(8,128)(2,1)} %all-gather.6.cloned.1.call-done.wqa), channel_id=1, source_target_pairs={{0,64},{64,0},{1,65},{65,1},{2,66},{66,2},{3,67},{67,3},{4,68},{68... | collective-permute-start | bytes 15728648 | tf_op jit(solution)/shard_map/ppermute | solution.py:471
  95.4 33.8 %copy-start.3 = (s32[1024]{0:T(1024)}, s32[1024]{0:T(1024)S(1)}, u32[]{:S(2)}) copy-start(s32[1024]{0:T(1024)S(1)} %multiply_add_fusion) | copy-start | bytes 12292
  121.2 144.5 %collective-permute-start.1 = (bf16[4,512,1024]{2,1,0:T(8,128)(2,1)}, bf16[4,512,1024]{2,1,0:T(8,128)(2,1)}, u32[]{:S(2)}, u32[]{:S(2)}) collective-permute-start(bf16[4,512,1024]{2,1,0:T(8,128)(2,1)} %all-gather.8.cloned.1.call-done.woa), channel_id=1, source_target_pairs={{0,64},{64,0},{1,65},{65,1},{2,66},{66,2},{3,67},{67,3},{4,68},{68... | collective-permute-start | bytes 12582920 | tf_op jit(solution)/shard_map/ppermute | solution.py:472
  134.6 0.8 copy-start.9
  135.4 8.2 %copy-start.5 = (f32[1280]{0:T(1024)S(1)}, f32[1280]{0:T(1024)}, u32[]{:S(2)}) copy-start(f32[1280]{0:T(1024)} %param.19) | copy-start | bytes 15364
  342.4 79.9 %copy-start.2 = (bf16[16,8192]{1,0:T(8,128)(2,1)S(1)}, bf16[16,8192]{1,0:T(8,128)(2,1)}, u32[]{:S(2)}) copy-start(bf16[16,8192]{1,0:T(8,128)(2,1)} %get-tuple-element.14) | copy-start | bytes 786436
Sparse Core Ops, SparseCore 0:
  11.1 59.4 all-gather.5
  72.3 48.8 all-gather.7
  122.9 57.2 all-gather.3

commit v2 on v1

v2 whole, which is shorter than its diff:
```python
import functools
import math

import jax
import jax.numpy as jnp
from jax import lax
from jax.experimental import pallas as pl
from jax.experimental.pallas import tpu as pltpu
from jax.sharding import PartitionSpec as P

QH = 32
KVH = 4
HD = 128
VD = 1280
VH = 16
VHD = 80
MERGE = 4
SIDE = 4
TOK = 128
FB = 512
HALF = TOK // 2
STEPS = (1, 3, 2)
HEADS = QH // KVH
QW = HEADS * HD
PW = QW + 2 * HD
PT = PW + HD
D = 8192
EPSILON = 1e-06
VMEM_LIMIT = 60 * 1024 * 1024
BF = jnp.bfloat16
F32 = jnp.float32


def layer_norm(values, norm_gain):
    values = values.astype(F32)
    centre = jnp.mean(values, axis=-1, keepdims=True)
    centred = values - centre
    variance = jnp.mean(centred * centred, axis=-1, keepdims=True)
    return centred * lax.rsqrt(variance + EPSILON) * norm_gain


def segment_of(lengths, amount):
    boundary = jnp.cumsum(lengths.astype(jnp.int32))
    positions = jnp.arange(amount, dtype=jnp.int32)
    return jnp.sum((positions[:, None] >= boundary[None, :]).astype(jnp.int32), axis=1)


def vision_rows(patches, units, v_gain, v_qkv, v_out, merge_gain):
    amount = patches.shape[0]
    merged_count = amount // MERGE
    unit_image = segment_of(units, merged_count)
    image_ids = jnp.broadcast_to(unit_image[:, None], (merged_count, MERGE)).reshape(amount)
    v_normed = layer_norm(patches, v_gain).astype(BF)
    projected = jnp.dot(v_normed, v_qkv, preferred_element_type=F32).astype(BF)
    projected = projected.reshape(amount, 3, VH, VHD)
    scores = jnp.einsum(
        "qhd,khd->hqk", projected[:, 0], projected[:, 1], preferred_element_type=F32
    ) / math.sqrt(VHD)
    allowed = image_ids[:, None] == image_ids[None, :]
    scores = jnp.where(allowed[None], scores, -1e30)
    weights = jax.nn.softmax(scores, axis=-1).astype(BF)
    attended = (
        jnp.einsum("hqk,khd->qhd", weights, projected[:, 2], preferred_element_type=F32)
        .astype(BF)
        .reshape(amount, VD)
    )
    update = jnp.dot(attended, v_out, preferred_element_type=F32)
    v_hidden = (patches.astype(F32) + update).astype(BF)
    merged = layer_norm(v_hidden, merge_gain).astype(BF)
    return merged.reshape(merged_count, MERGE * VD)


def push(src, dst, send_sem, recv_sem, where):
    copy = pltpu.make_async_remote_copy(
        src_ref=src,
        dst_ref=dst,
        send_sem=send_sem,
        recv_sem=recv_sem,
        device_id=where,
        device_id_type=pl.DeviceIdType.MESH,
    )
    copy.start()
    return copy


def greet(partners):
    barrier = pltpu.get_barrier_semaphore()
    for where in partners:
        pl.semaphore_signal(
            barrier, inc=1, device_id=where, device_id_type=pl.DeviceIdType.MESH
        )
    pl.semaphore_wait(barrier, len(partners))


def along(index, step):
    return lax.rem(index + step, SIDE)


def behind(index, step):
    return lax.rem(index + SIDE - step, SIDE)


def merge_kernel(
    pieces, wm, text, lslot,
    h0,
    wmv, xbuf, part, psend, rbuf, ybuf, tbuf, pick,
    w_sem, s_w, r_w, s_pl, r_pl, s_x, r_x, s_y, r_y, s_t, r_t,
):
    section = lax.axis_index("section")
    x = lax.axis_index("x")
    y = lax.axis_index("y")
    z = lax.axis_index("mp")
    plane = [(dx, dz) for dx in range(SIDE) for dz in range(SIDE) if dx or dz]
    half = wm.shape[1]

    for block in range(SIDE):
        pltpu.make_async_copy(wm.at[block], wmv.at[block, section], w_sem.at[block]).start()
    greet(
        [{"x": along(x, dx), "mp": along(z, dz)} for dx, dz in plane]
        + [{"y": along(y, dy)} for dy in STEPS]
        + [{"section": 1 - section}]
    )
    plane_copies = []
    for dx, dz in plane:
        xt = along(x, dx)
        plane_copies.append(
            push(
                pieces.at[xt], xbuf.at[x * SIDE + z],
                s_pl.at[dx * SIDE + dz], r_pl.at[dx * SIDE + dz],
                {"x": xt, "mp": along(z, dz)},
            )
        )
    xbuf[x * SIDE + z] = pieces[x]
    twin_copies = [
        push(
            wm.at[block], wmv.at[block, section], s_w.at[block], r_w.at[block],
            {"section": 1 - section},
        )
        for block in range(SIDE)
    ]
    text_copies = []
    for dx in STEPS:
        xt = along(x, dx)
        text_copies.append(
            push(
                text.at[:, pl.ds(pl.multiple_of(xt * FB, FB), FB)], tbuf.at[x],
                s_t.at[dx], r_t.at[dx], {"x": xt},
            )
        )
    tbuf[x] = text[:, pl.ds(pl.multiple_of(x * FB, FB), FB)]

    slots = lslot[...]
    for block in range(SIDE):
        wanted = lax.broadcasted_iota(jnp.int32, (TOK, slots.shape[1]), 0) + block * TOK
        pick[pl.ds(block * TOK, TOK), :] = jnp.where(wanted == slots, 1.0, 0.0).astype(BF)

    for block in range(SIDE):
        pltpu.make_async_copy(wm.at[block], wmv.at[block, section], w_sem.at[block]).wait()
    for copy in twin_copies:
        copy.wait()
    for copy in plane_copies:
        copy.wait()

    def product(dx):
        cols = pl.ds(pl.multiple_of(along(x, dx) * FB, FB), FB)
        rows = xbuf[...].reshape(SIDE * SIDE * 16, VD)
        weights = wmv[:, :, :, cols].reshape(SIDE * 2 * half, FB)
        return jnp.dot(rows, weights, preferred_element_type=F32)

    x_copies = []
    for dx in STEPS:
        psend[dx] = product(dx).astype(BF)
        x_copies.append(
            push(psend.at[dx], rbuf.at[dx], s_x.at[dx], r_x.at[dx], {"x": along(x, dx)})
        )
    part[...] = product(0)
    for copy in x_copies:
        copy.wait()
    total = part[...]
    for dx in STEPS:
        total = total + rbuf[dx].astype(F32)
    ybuf[y] = total.astype(BF)
    y_copies = [
        push(ybuf.at[y], ybuf.at[y], s_y.at[dy], r_y.at[dy], {"y": along(y, dy)})
        for dy in STEPS
    ]
    chosen = pick[...]
    present = jnp.dot(chosen, jnp.ones((SIDE * 256, 128), BF), preferred_element_type=F32)
    for copy in text_copies:
        copy.wait()
    for copy in y_copies:
        copy.wait()
    picked = jnp.dot(
        chosen, ybuf[...].reshape(SIDE * 256, FB), preferred_element_type=F32
    ).astype(BF)
    for group in range(SIDE):
        for part_of in range(2):
            rows = slice(group * TOK + part_of * HALF, group * TOK + (part_of + 1) * HALF)
            to = slice(group * HALF, (group + 1) * HALF)
            inside = slice(part_of * HALF, (part_of + 1) * HALF)
            for tile in range(FB // 128):
                cols = slice(tile * 128, (tile + 1) * 128)
                h0[part_of, to, cols] = jnp.where(
                    present[rows, :] > 0.5, picked[rows, cols], tbuf[group, inside, cols]
                )


def merge_call(pieces, wm, text, lslot):
    vmem = pl.BlockSpec(memory_space=pltpu.VMEM)
    dma = pltpu.SemaphoreType.DMA
    half = wm.shape[1]
    return pl.pallas_call(
        merge_kernel,
        out_shape=jax.ShapeDtypeStruct((2, SIDE * HALF, FB), BF),
        in_specs=[vmem, pl.BlockSpec(memory_space=pl.ANY), vmem, vmem],
        out_specs=vmem,
        scratch_shapes=[
            pltpu.VMEM((SIDE, 2, half, SIDE * FB), BF),
            pltpu.VMEM((SIDE * SIDE, 16, VD), BF),
            pltpu.VMEM((256, FB), F32),
            pltpu.VMEM((SIDE, 256, FB), BF),
            pltpu.VMEM((SIDE, 256, FB), BF),
            pltpu.VMEM((SIDE, 256, FB), BF),
            pltpu.VMEM((SIDE, TOK, FB), BF),
            pltpu.VMEM((SIDE * TOK, 1024), BF),
            dma((SIDE,)),
            dma((SIDE,)), dma((SIDE,)),
            dma((16,)), dma((16,)),
            dma((SIDE,)), dma((SIDE,)),
            dma((SIDE,)), dma((SIDE,)),
            dma((SIDE,)), dma((SIDE,)),
        ],
        compiler_params=pltpu.CompilerParams(
            collective_id=1, has_side_effects=True, vmem_limit_bytes=VMEM_LIMIT
        ),
        name="merge",
    )(pieces, wm, text, lslot)


def layers_kernel(
    h, w_first, w_mine, mask, gslot, grads,
    out, mg,
    w, zbuf, acc, squares, kv, psend, rbuf, abuf, osend, orec, obuf,
    gbuf, gsend, grec, gz, mz,
    w_sem, s_w0, r_w0, s_w1, r_w1, s_w2, r_w2,
    s_z, r_z, s_x, r_x, s_a, r_a, s_o, r_o, s_e, r_e,
    s_g, r_g, s_gx, r_gx, s_gz, r_gz,
):
    section = lax.axis_index("section")
    x = lax.axis_index("x")
    y = lax.axis_index("y")
    z = lax.axis_index("mp")
    twin = {"section": 1 - section}
    rows = SIDE * HALF
    half = FB // 2
    width = grads.shape[1]
    mine = pl.ds(pl.multiple_of(section * half, half), half)

    own_load = pltpu.make_async_copy(w_first, w.at[0, :, mine, :], w_sem.at[0])
    own_load.start()
    own_shard = pltpu.make_async_copy(w_mine, w.at[1, y], w_sem.at[1])
    for part in range(2):
        zbuf[0, part, z] = h[part]
    greet(
        [{"x": along(x, d)} for d in STEPS]
        + [{"mp": along(z, d)} for d in STEPS]
        + [{"y": along(y, d)} for d in STEPS]
        + [twin]
    )

    z_copies, x_copies, a_copies, o_copies, e_copies = {}, {}, {}, {}, []

    def spread(layer, part):
        z_copies[layer, part] = {
            dz: push(
                zbuf.at[layer, part, z], zbuf.at[layer, part, z],
                s_z.at[layer, part, dz], r_z.at[layer, part, dz], {"mp": along(z, dz)},
            )
            for dz in STEPS
        }

    def project(layer, part):
        for dz in (0, 1, 3, 2):
            zs = behind(z, dz)
            if dz:
                z_copies[layer, part][dz].wait()
            wide = zbuf[layer, part, zs].astype(F32)
            squared = jnp.sum(wide * wide, axis=1, keepdims=True)
            if dz:
                squares[part] += jnp.broadcast_to(squared, (rows, HD))
            else:
                squares[part] = jnp.broadcast_to(squared, (rows, HD))

            @pl.loop(0, PW // 256)
            def _(tile):
                cols = pl.ds(pl.multiple_of(tile * 256, 256), 256)
                product = jnp.dot(
                    zbuf[layer, part, zs], w[layer, zs, :, cols], preferred_element_type=F32
                )
                if dz:
                    acc[part, :, cols] += product
                else:
                    acc[part, :, cols] = product

        lane = lax.broadcasted_iota(jnp.int32, (HALF, HD), 1)
        copies = []
        for dx in STEPS:
            xt = along(x, dx)
            span = pl.ds(pl.multiple_of(xt * HALF, HALF), HALF)
            psend[layer, part, dx, :, :PW] = acc[part, span, :].astype(BF)
            sq = squares[part, span, :]
            high = sq.astype(BF)
            low = (sq - high.astype(F32)).astype(BF)
            psend[layer, part, dx, :, PW:] = jnp.where(lane < 64, high, low)
            copies.append(
                push(
                    psend.at[layer, part, dx], rbuf.at[layer, part, dx],
                    s_x.at[layer, part, dx], r_x.at[layer, part, dx], {"x": xt},
                )
            )
        x_copies[layer, part] = copies

    def attend(layer, part):
        own = pl.ds(pl.multiple_of(x * HALF, HALF), HALF)
        total = acc[part, own, :]
        sq = squares[part, own, :][:, :1]
        for copy in x_copies[layer, part]:
            copy.wait()
        for dx in STEPS:
            total = total + rbuf[layer, part, dx, :, :PW].astype(F32)
            tail = rbuf[layer, part, dx, :, PW:].astype(F32)
            sq = sq + tail[:, :1] + tail[:, 64:65]
        projected = (total * lax.rsqrt(sq / D + EPSILON)).astype(BF)
        kv[part * HALF : (part + 1) * HALF, :] = projected[:, QW:]
        seen = (part + 1) * HALF
        keys = kv[:seen, :HD]
        values = kv[:seen, HD:]
        queries = jnp.concatenate(
            [projected[:, head * HD : (head + 1) * HD] for head in range(HEADS)], axis=0
        )
        allowed = mask[part * HALF : (part + 1) * HALF, :seen]
        allowed = jnp.concatenate([allowed] * HEADS, axis=0) > 0.5
        scores = lax.dot_general(
            queries, keys, (((1,), (1,)), ((), ())), preferred_element_type=F32
        ) * (1.0 / math.sqrt(HD))
        scores = jnp.where(allowed, scores, -1e30)
        top = jnp.max(scores, axis=1, keepdims=True)
        weights = jnp.exp(scores - top)
        weights = (weights / jnp.sum(weights, axis=1, keepdims=True)).astype(BF)
        mixed = jnp.dot(weights, values, preferred_element_type=F32).astype(BF)
        for head in range(HEADS):
            abuf[layer, part, x, :, head * HD : (head + 1) * HD] = mixed[
                head * HALF : (head + 1) * HALF, :
            ]
        a_copies[layer, part] = [
            push(
                abuf.at[layer, part, x], abuf.at[layer, part, x],
                s_a.at[layer, part, dx], r_a.at[layer, part, dx], {"x": along(x, dx)},
            )
            for dx in STEPS
        ]

    def output(layer, part):
        for copy in a_copies[layer, part]:
            copy.wait()
        copies = []
        for dz in (1, 3, 2, 0):
            zt = along(z, dz)

            @pl.loop(0, FB // 256)
            def _(tile):
                cols = pl.ds(pl.multiple_of(tile * 256, 256), 256)
                osend[layer, part, dz, :, cols] = lax.dot_general(
                    abuf[layer, part].reshape(rows, QW), w[layer, zt, cols, PW:],
                    (((1,), (1,)), ((), ())), preferred_element_type=F32,
                ).astype(BF)

            if dz:
                copies.append(
                    push(
                        osend.at[layer, part, dz], orec.at[layer, part, dz],
                        s_o.at[layer, part, dz], r_o.at[layer, part, dz], {"mp": zt},
                    )
                )
        o_copies[layer, part] = copies

    def finish(layer, part):
        update = osend[layer, part, 0].astype(F32)
        for copy in o_copies[layer, part]:
            copy.wait()
        for dz in STEPS:
            update = update + orec[layer, part, dz].astype(F32)
        fresh = (zbuf[layer, part, z].astype(F32) + update).astype(BF)
        if layer == 0:
            zbuf[1, part, z] = fresh
            return
        osend[layer, part, 0] = fresh
        for dx in STEPS:
            xt = along(x, dx)
            e_copies.append(
                push(
                    osend.at[layer, part, 0, pl.ds(pl.multiple_of(xt * HALF, HALF), HALF), :],
                    obuf.at[x, part],
                    s_e.at[part, dx], r_e.at[part, dx], {"x": xt},
                )
            )
        obuf[x, part] = osend[
            layer, part, 0, pl.ds(pl.multiple_of(x * HALF, HALF), HALF), :
        ]

    spread(0, 0)
    spread(0, 1)
    twin_copy = push(w_first, w.at[0, :, mine, :], s_w0.at[0], r_w0.at[0], twin)

    def shard_copy(dy):
        return pltpu.make_async_remote_copy(
            src_ref=w_mine, dst_ref=w.at[1, y], send_sem=s_w1.at[dy], recv_sem=r_w1.at[dy],
            device_id={"y": along(y, dy)}, device_id_type=pl.DeviceIdType.MESH,
        )

    def forward_copy(dy):
        ys = behind(y, dy)
        return pltpu.make_async_remote_copy(
            src_ref=w.at[1, ys], dst_ref=w.at[1, ys], send_sem=s_w2.at[dy],
            recv_sem=r_w2.at[dy], device_id=twin, device_id_type=pl.DeviceIdType.MESH,
        )

    @pl.when(section == 1)
    def _():
        for dy in STEPS:
            shard_copy(dy).start()
        own_shard.start()

    own_load.wait()
    twin_copy.wait()
    project(0, 0)
    project(0, 1)
    attend(0, 0)
    attend(0, 1)
    g_copies = [
        push(grads, gbuf.at[y], s_g.at[dy], r_g.at[dy], {"y": along(y, dy)}) for dy in STEPS
    ]
    gbuf[y] = grads[...]
    output(0, 0)
    output(0, 1)

    @pl.when(section == 1)
    def _():
        own_shard.wait()
        forward_copy(0).start()
        for dy in STEPS:
            shard_copy(dy).wait()
            forward_copy(dy).start()

    finish(0, 0)
    spread(1, 0)
    finish(0, 1)
    spread(1, 1)

    @pl.when(section == 0)
    def _():
        for dy in range(SIDE):
            forward_copy(dy).wait_recv()

    project(1, 0)
    project(1, 1)
    attend(1, 0)
    attend(1, 1)

    for copy in g_copies:
        copy.wait()
    gx_copies = []
    for dx in (1, 3, 2, 0):
        xt = along(x, dx)
        wanted = gslot[pl.ds(pl.multiple_of(xt * 64, 64), 64), :]
        lanes = lax.broadcasted_iota(jnp.int32, (64, SIDE * TOK), 1)
        chosen = jnp.where(lanes == wanted, 1.0, 0.0).astype(BF)
        gsend[dx] = jnp.dot(
            chosen, gbuf[...].reshape(SIDE * TOK, width), preferred_element_type=F32
        ).astype(BF)
        if dx:
            gx_copies.append(
                push(gsend.at[dx], grec.at[dx], s_gx.at[dx], r_gx.at[dx], {"x": xt})
            )

    output(1, 0)
    output(1, 1)
    for copy in gx_copies:
        copy.wait()
    found = gsend[0].astype(F32)
    for dx in STEPS:
        found = found + grec[dx].astype(F32)
    gz[...] = found.astype(BF).reshape(SIDE, 16, width)
    gz_copies = []
    for dz in STEPS:
        zt = along(z, dz)
        gz_copies.append(push(gz.at[zt], mz.at[z], s_gz.at[dz], r_gz.at[dz], {"mp": zt}))
    mz[z] = gz[z]

    finish(1, 0)
    finish(1, 1)
    for copy in gz_copies:
        copy.wait()
    for block in range(SIDE):
        mg[:, block * width : (block + 1) * width] = mz[block]
    for copy in e_copies:
        copy.wait()
    for block in range(SIDE):
        for part in range(2):
            out[part * HALF : (part + 1) * HALF, block * FB : (block + 1) * FB] = obuf[block, part]

    @pl.when(section == 1)
    def _():
        for dy in range(SIDE):
            forward_copy(dy).wait_send()


def layers_call(h, w_first, w_mine, mask, gslot, grads):
    vmem = pl.BlockSpec(memory_space=pltpu.VMEM)
    hbm = pl.BlockSpec(memory_space=pl.ANY)
    dma = pltpu.SemaphoreType.DMA
    rows = SIDE * HALF
    width = grads.shape[1]
    stage = dma((2, 2, SIDE))
    return pl.pallas_call(
        layers_kernel,
        out_shape=(
            jax.ShapeDtypeStruct((TOK, SIDE * FB), BF),
            jax.ShapeDtypeStruct((16, SIDE * width), BF),
        ),
        in_specs=[vmem, hbm, hbm, vmem, vmem, vmem],
        out_specs=(vmem, vmem),
        scratch_shapes=[
            pltpu.VMEM((2, SIDE, FB, PW + QW), BF),
            pltpu.VMEM((2, 2, SIDE, rows, FB), BF),
            pltpu.VMEM((2, rows, PW), F32),
            pltpu.VMEM((2, rows, HD), F32),
            pltpu.VMEM((TOK, 2 * HD), BF),
            pltpu.VMEM((2, 2, SIDE, HALF, PT), BF),
            pltpu.VMEM((2, 2, SIDE, HALF, PT), BF),
            pltpu.VMEM((2, 2, SIDE, HALF, QW), BF),
            pltpu.VMEM((2, 2, SIDE, rows, FB), BF),
            pltpu.VMEM((2, 2, SIDE, rows, FB), BF),
            pltpu.VMEM((SIDE, 2, HALF, FB), BF),
            pltpu.VMEM((SIDE, TOK, width), BF),
            pltpu.VMEM((SIDE, 64, width), BF),
            pltpu.VMEM((SIDE, 64, width), BF),
            pltpu.VMEM((SIDE, 16, width), BF),
            pltpu.VMEM((SIDE, 16, width), BF),
            dma((2,)),
            dma((1,)), dma((1,)),
            dma((SIDE,)), dma((SIDE,)),
            dma((SIDE,)), dma((SIDE,)),
            stage, stage,
            stage, stage,
            stage, stage,
            stage, stage,
            dma((2, SIDE)), dma((2, SIDE)),
            dma((SIDE,)), dma((SIDE,)),
            dma((SIDE,)), dma((SIDE,)),
            dma((SIDE,)), dma((SIDE,)),
        ],
        compiler_params=pltpu.CompilerParams(
            collective_id=2, has_side_effects=True, vmem_limit_bytes=VMEM_LIMIT
        ),
        name="layers",
    )(h, w_first, w_mine, mask, gslot, grads)


def shards(
    patches,
    image_units,
    v_gain,
    v_qkv,
    v_out,
    merge_gain,
    w_merge,
    routes,
    text,
    seq_lengths,
    lang_gain,
    w_qkv,
    wo_t,
    row_grads,
):
    section = lax.axis_index("section")
    x = lax.axis_index("x")
    y = lax.axis_index("y")

    sent = lax.optimization_barrier(jnp.broadcast_to(routes, (routes.shape[0], 128)))
    target = lax.optimization_barrier(
        lax.all_gather(sent, ("y", "x", "mp"), axis=0, tiled=True)
    )[:, 0]
    part = w_merge.shape[0] // 2
    wm = lax.all_gather(
        lax.dynamic_slice_in_dim(w_merge, section * part, part, 0), "y", axis=0, tiled=False
    )
    gain = lax.dynamic_slice_in_dim(lang_gain[0], (y * SIDE + x) * FB, FB, 0)
    scaled = (w_qkv[0].astype(F32) * gain[:, None]).astype(BF)
    w_mine = jnp.concatenate([scaled, wo_t[0]], axis=1)
    swapped = lax.ppermute(w_mine[FB // 2 :], "section", [(0, 1)])
    w_half = jnp.where(section == 0, w_mine[: FB // 2], swapped)
    w_first = lax.all_gather(w_half, "y", axis=0, tiled=False)

    count = target.shape[0]
    order = jnp.arange(count, dtype=jnp.int32)
    position = jnp.sum(
        ((target[:, None] == target[None, :]) & (order[:, None] > order[None, :])).astype(jnp.int32),
        axis=1,
    )
    lslot = (target - y * SIDE) * TOK + position
    gslot = jnp.where(target % SIDE == x, (target // SIDE) * TOK + position, -1)
    gslot = lax.dynamic_slice_in_dim(gslot, y * 256, 256, 0)

    merged = vision_rows(patches, image_units[0], v_gain, v_qkv, v_out, merge_gain)
    pieces = merged.reshape(16, MERGE, SIDE, 320).transpose(2, 0, 1, 3).reshape(SIDE, 16, VD)
    seq = segment_of(seq_lengths[0], TOK)
    at = jnp.arange(TOK, dtype=jnp.int32)
    mask = ((seq[:, None] == seq[None, :]) & (at[:, None] >= at[None, :])).astype(F32)

    hidden = merge_call(pieces, wm, text, lslot[None, :])
    return layers_call(hidden, w_first, w_mine, mask, gslot[:, None], row_grads)


def solution(mesh):
    grid = jax.sharding.Mesh(
        mesh.devices.reshape(2, SIDE, SIDE, SIDE), ("section", "y", "x", "mp")
    )
    every = ("section", "y", "x", "mp")
    home = P(("section", "y", "x"), "mp")
    in_specs = (
        P(every, None),
        P(every, None),
        P(),
        P(),
        P(),
        P(),
        P(("y", "x"), "mp"),
        P(every, None),
        home,
        P(("section", "y", "x"), None),
        P("section", None),
        P("section", ("y", "x"), "mp"),
        P("section", ("y", "x"), "mp"),
        home,
    )
    out_specs = (home, P(every, None))
    return jax.shard_map(shards, mesh=grid, in_specs=in_specs, out_specs=out_specs, check_vma=False)
```

time: 430 us -> 445 us (1.035)
  blocking collectives: 22.4 us -> 191 us
  waiting for transfers between devices: 116 us -> 1.8 us
  Pallas kernels: 240 us -> 188 us
  other arithmetic: 5.53 us -> 13.9 us
    all_gather x0 -> x1, blocking collectives: none -> 191 us  [shards(): lax.all_gather(sent, ('y', 'x', 'mp'), axis=0, tiled=True)]
    all_gather x3 -> x2, waiting for transfers between devices: 115 us -> 0.02 us  [the longest x1 0.02 us: shards(): w_first = lax.all_gather(w_half, 'y', axis=0, tiled=False)]
    pallas_call x3 -> x2, Pallas kernels: 240 us -> 188 us  [the longest x1 147 us: layers_call(): pl.pallas_call(layers_kernel, out_shape=(jax.ShapeDtypeStruct((TOK, SIDE...]
    eq x1 -> x0, blocking collectives: 22.4 us -> none  [shards(): target[:, None] == target[None, :]]
  transfers between devices with their start and end apart: 5 -> 3, of which waited for: 3 -> 1; matrix products, arithmetic and copies ran while one was open for 7% -> 9% of each run, Pallas kernels for 20% -> 9%
where the time goes in v2:
time: 445 us; the launch traced here: 444 us
  blocking collectives  191 us (43%)
  Pallas kernels  188 us (42%)
  local copies, waits for them, and re-layouts  22 us (5%)
  between operations  14.2 us (3%)
  other arithmetic  13.9 us (3%)
  matrix products  11.3 us (3%)
    all_gather x1, blocking collectives, shards(): lax.all_gather(sent, ('y', 'x', 'mp'), axis=0, tiled=True)  191 us
    pallas_call x1, Pallas kernels, layers_call(): pl.pallas_call(layers_kernel, out_shape=(jax.ShapeDtypeStruct((TOK, SIDE...  147 us
    pallas_call x1, Pallas kernels, merge_call(): pl.pallas_call(merge_kernel, out_shape=jax.ShapeDtypeStruct((2, SIDE * HA...  40.3 us
  transfers between devices with their start and end apart: 3, of which 1 were waited for; matrix products, arithmetic and copies ran while one was open for 9% of the time, Pallas kernels for 9%

profile of v2, /device:TPU:0, one launch (start us, length us, event | category | flops | bytes accessed | tf_op | source)
XLA Modules:
  0.0 444.5 jit_solution(6788886045311384171)
XLA Ops:
  7.2 2.1 constant_dynamic-slice_fusion.1
  10.2 1.6 fusion.2
  11.9 1.1 copy-done.1
  12.9 1.2 fusion.10
  14.1 2.3 collective-permute-start
  16.5 1.7 collective-permute-done
  18.2 2.5 fusion.9
  21.1 6.9 %convolution_convert_fusion = bf16[64,3840]{1,0:T(8,128)(2,1)} fusion(bf16[1280,3840]{1,0:T(8,128)(2,1)} %param.17, bf16[64,1280]{1,0:T(8,128)(2,1)S(1)} %copy-done.3, f32[1280]{0:T(1024)S(1)} %copy-done.4, f32[64]{0:T(128)S(1)} %add_rsqrt_fusion.1, f32[64]{0:T(128)S(1)} %broadcast_multiply_fusion.1), kind=kOutput, calls=%fused_computation.1 | convolution fusion | flops 629800960 | bytes 10491392 | tf_op jit(solution)/shard_map/dot_general | solution.py:54
  28.0 3.0 reshape.155
  31.6 2.0 fusion.31
  34.8 2.4 fusion.11
  37.2 1.8 copy.39
  39.0 1.9 reshape.158
  40.9 1.7 fusion.33
  43.7 1.1 reshape_reshape.3
  45.6 1.8 reshape.159.pieces
  47.5 191.2 %all_gather.17 = s32[1024,128]{1,0:T(8,128)} all-gather(s32[16,128]{1,0:T(8,128)S(1)} %broadcast_in_dim.26), channel_id=1, replica_groups=mesh['section'=2,'y'=4,'x'=4,'mp'=4] {'y','x','mp'}, dimensions={0}, use_global_device_ids=true | all-gather | bytes 532480 | tf_op jit(solution)/shard_map/all_gather | solution.py:592
  238.7 1.4 slice_reduce_fusion
  240.7 0.8 copy.41.gslot
  243.1 3.3 pad_maximum_fusion.w_mine
  246.4 40.3 %merge.1.h = bf16[2,256,512]{2,1,0:T(8,128)(2,1)} custom-call(bf16[4,16,1280]{2,1,0:T(8,128)(2,1)} %reshape.159.pieces, bf16[4,160,2048]{2,1,0:T(8,128)(2,1)} %bitcast.38, bf16[128,2048]{1,0:T(8,128)(2,1)} %text.1, s32[1,1024]{1,0:T(1,128)} %add.55.lslot), custom_call_target="tpu_custom_call" | custom-call | tf_op jit(solution)/shard_map/merge/pallas_call | solution.py:212
  286.7 147.3 %layers.1 = (bf16[128,2048]{1,0:T(8,128)(2,1)}, bf16[16,8192]{1,0:T(8,128)(2,1)}) custom-call(bf16[2,256,512]{2,1,0:T(8,128)(2,1)} %merge.1.h, bf16[4,256,2304]{2,1,0:T(8,128)(2,1)} %bitcast.37, bf16[512,2304]{1,0:T(8,128)(2,1)} %pad_maximum_fusion.w_mine, f32[128,128]{1,0:T(8,128)} %fusion.23.mask, s32[256,1]{1,0:T(8,128)} %copy.41.gslot, ...), custom_call_target="tpu_custom_call" | custom-call | tf_op jit(solution)/shard_map/layers/pallas_call | solution.py:525
  434.1 1.9 copy.56
  436.0 1.7 copy.57
  (50 shorter events, 7.0 us)
Async XLA Ops:
  7.2 33.8 %copy-start = (bf16[1280,1280]{1,0:T(8,128)(2,1)S(1)}, bf16[1280,1280]{1,0:T(8,128)(2,1)}, u32[]{:S(2)}) copy-start(bf16[1280,1280]{1,0:T(8,128)(2,1)} %param.18) | copy-start | bytes 9830404
  7.2 239.2 %all-gather.5.cloned.1.call-start = ((), (), s32[]{:S(2)}) async-start(), calls=%async_computation | async-start | bytes 3276800 | tf_op jit(solution)/shard_map/all_gather | solution.py:595
  9.4 277.3 %all-gather.7.cloned.1.call-start = ((), (), s32[]{:S(2)}) async-start(), calls=%async_computation.1 | async-start | bytes 5898240 | tf_op jit(solution)/shard_map/all_gather | solution.py:603
  9.5 3.5 copy-start.2
  11.8 1.1 copy-start.1
  14.1 4.1 collective-permute-start
  16.5 4.3 copy-start.3
  16.5 4.7 %copy-start.4 = (f32[1280]{0:T(1024)S(1)}, f32[1280]{0:T(1024)}, u32[]{:S(2)}) copy-start(f32[1280]{0:T(1024)} %param.16) | copy-start | bytes 15364
  21.1 9.9 %copy-start.7 = (s32[1,3]{1,0:T(1,128)S(1)}, s32[1,3]{1,0:T(1,128)}, u32[]{:S(2)}) copy-start(s32[1,3]{1,0:T(1,128)} %param.15) | copy-start | bytes 40
  33.8 0.8 copy-start.9
  39.0 3.9 copy-start.5
  40.9 6.5 %copy-start.6 = (s32[16,1]{0,1:T(1,128)S(1)}, s32[16,1]{0,1:T(1,128)}, u32[]{:S(2)}) copy-start(s32[16,1]{0,1:T(1,128)} %param.21) | copy-start | bytes 196
  42.7 198.9 %copy-start.8 = (s32[1,3]{1,0:T(1,128)S(1)}, s32[1,3]{1,0:T(1,128)}, u32[]{:S(2)}) copy-start(s32[1,3]{1,0:T(1,128)} %param.23) | copy-start | bytes 40
Sparse Core Ops, SparseCore 0:
  9.7 37.7 all-gather.4
  49.1 52.6 all-gather.6

commit v3 on v2

--- a/solution.py
+++ b/solution.py
@@ -101,10 +101,10 @@
 
 
 def merge_kernel(
-    pieces, wm, text, lslot,
-    h0,
-    wmv, xbuf, part, psend, rbuf, ybuf, tbuf, pick,
-    w_sem, s_w, r_w, s_pl, r_pl, s_x, r_x, s_y, r_y, s_t, r_t,
+    pieces, wm, text, placed,
+    h0, gslot,
+    wmv, xbuf, part, psend, rbuf, ybuf, tbuf, pick, rt, ry, tri, line,
+    w_sem, s_w, r_w, s_pl, r_pl, s_x, r_x, s_y, r_y, s_t, r_t, s_rt, r_rt, s_ry, r_ry,
 ):
     section = lax.axis_index("section")
     x = lax.axis_index("x")
@@ -120,6 +120,14 @@
         + [{"y": along(y, dy)} for dy in STEPS]
         + [{"section": 1 - section}]
     )
+    route_copies = [
+        push(
+            placed, rt.at[x * SIDE + z], s_rt.at[dx * SIDE + dz], r_rt.at[dx * SIDE + dz],
+            {"x": along(x, dx), "mp": along(z, dz)},
+        )
+        for dx, dz in plane
+    ]
+    rt[x * SIDE + z] = placed[...]
     plane_copies = []
     for dx, dz in plane:
         xt = along(x, dx)
@@ -149,10 +157,21 @@
         )
     tbuf[x] = text[:, pl.ds(pl.multiple_of(x * FB, FB), FB)]
 
-    slots = lslot[...]
+    count = tri.shape[0]
     for block in range(SIDE):
-        wanted = lax.broadcasted_iota(jnp.int32, (TOK, slots.shape[1]), 0) + block * TOK
-        pick[pl.ds(block * TOK, TOK), :] = jnp.where(wanted == slots, 1.0, 0.0).astype(BF)
+        before = lax.broadcasted_iota(jnp.int32, (256, count), 0) + block * 256
+        after = lax.broadcasted_iota(jnp.int32, (256, count), 1)
+        tri[block * 256 : (block + 1) * 256, :] = jnp.where(before < after, 1.0, 0.0).astype(BF)
+    for copy in route_copies:
+        copy.wait()
+    known = rt[0]
+    for source in range(1, SIDE * SIDE):
+        known = known + rt[source]
+    ry[y] = known
+    ry_copies = [
+        push(ry.at[y], ry.at[y], s_ry.at[dy], r_ry.at[dy], {"y": along(y, dy)})
+        for dy in STEPS
+    ]
 
     for block in range(SIDE):
         pltpu.make_async_copy(wm.at[block], wmv.at[block, section], w_sem.at[block]).wait()
@@ -174,6 +193,32 @@
             push(psend.at[dx], rbuf.at[dx], s_x.at[dx], r_x.at[dx], {"x": along(x, dx)})
         )
     part[...] = product(0)
+
+    for copy in ry_copies:
+        copy.wait()
+    target = ry[0] + ry[1] + ry[2] + ry[3]
+    groups = lax.broadcasted_iota(jnp.int32, (SIDE * SIDE, count), 0)
+    named = jnp.where(groups == target, 1.0, 0.0)
+    earlier = jnp.dot(named.astype(BF), tri[...], preferred_element_type=F32)
+    position = jnp.sum(named * earlier, axis=0, keepdims=True).astype(jnp.int32)
+    slots = (target - y * SIDE) * TOK + position
+    for block in range(SIDE):
+        wanted = lax.broadcasted_iota(jnp.int32, (TOK, count), 0) + block * TOK
+        pick[pl.ds(block * TOK, TOK), :] = jnp.where(wanted == slots, 1.0, 0.0).astype(BF)
+    line[...] = jnp.where((target & 3) == x, (target >> 2) * TOK + position + 1, 0)
+    returned = line[:, pl.ds(pl.multiple_of(y * 256, 256), 256)]
+    across = lax.broadcasted_iota(jnp.int32, (256, 256), 1)
+    down = lax.broadcasted_iota(jnp.int32, (256, 256), 0)
+    same = jnp.where(across == down, 1.0, 0.0).astype(BF)
+
+    def upright(row):
+        wide = jnp.broadcast_to(row.astype(F32), (128, 256)).astype(BF)
+        return lax.dot_general(
+            same, wide, (((1,), (1,)), ((), ())), preferred_element_type=F32
+        )
+
+    gslot[...] = (16.0 * upright(returned >> 4) + upright(returned & 15)).astype(jnp.int32) - 1
+
     for copy in x_copies:
         copy.wait()
     total = part[...]
@@ -205,15 +250,18 @@
                 )
 
 
-def merge_call(pieces, wm, text, lslot):
+def merge_call(pieces, wm, text, placed):
     vmem = pl.BlockSpec(memory_space=pltpu.VMEM)
     dma = pltpu.SemaphoreType.DMA
     half = wm.shape[1]
     return pl.pallas_call(
         merge_kernel,
-        out_shape=jax.ShapeDtypeStruct((2, SIDE * HALF, FB), BF),
+        out_shape=(
+            jax.ShapeDtypeStruct((2, SIDE * HALF, FB), BF),
+            jax.ShapeDtypeStruct((256, 128), jnp.int32),
+        ),
         in_specs=[vmem, pl.BlockSpec(memory_space=pl.ANY), vmem, vmem],
-        out_specs=vmem,
+        out_specs=(vmem, vmem),
         scratch_shapes=[
             pltpu.VMEM((SIDE, 2, half, SIDE * FB), BF),
             pltpu.VMEM((SIDE * SIDE, 16, VD), BF),
@@ -223,18 +271,24 @@
             pltpu.VMEM((SIDE, 256, FB), BF),
             pltpu.VMEM((SIDE, TOK, FB), BF),
             pltpu.VMEM((SIDE * TOK, 1024), BF),
+            pltpu.VMEM((SIDE * SIDE, 1, 1024), jnp.int32),
+            pltpu.VMEM((SIDE, 1, 1024), jnp.int32),
+            pltpu.VMEM((1024, 1024), BF),
+            pltpu.VMEM((1, 1024), jnp.int32),
             dma((SIDE,)),
             dma((SIDE,)), dma((SIDE,)),
             dma((16,)), dma((16,)),
             dma((SIDE,)), dma((SIDE,)),
             dma((SIDE,)), dma((SIDE,)),
+            dma((SIDE,)), dma((SIDE,)),
+            dma((16,)), dma((16,)),
             dma((SIDE,)), dma((SIDE,)),
         ],
         compiler_params=pltpu.CompilerParams(
             collective_id=1, has_side_effects=True, vmem_limit_bytes=VMEM_LIMIT
         ),
         name="merge",
-    )(pieces, wm, text, lslot)
+    )(pieces, wm, text, placed)
 
 
 def layers_kernel(
@@ -472,7 +526,7 @@
     gx_copies = []
     for dx in (1, 3, 2, 0):
         xt = along(x, dx)
-        wanted = gslot[pl.ds(pl.multiple_of(xt * 64, 64), 64), :]
+        wanted = gslot[pl.ds(pl.multiple_of(xt * 64, 64), 64), :1]
         lanes = lax.broadcasted_iota(jnp.int32, (64, SIDE * TOK), 1)
         chosen = jnp.where(lanes == wanted, 1.0, 0.0).astype(BF)
         gsend[dx] = jnp.dot(
@@ -587,10 +641,6 @@
     x = lax.axis_index("x")
     y = lax.axis_index("y")
 
-    sent = lax.optimization_barrier(jnp.broadcast_to(routes, (routes.shape[0], 128)))
-    target = lax.optimization_barrier(
-        lax.all_gather(sent, ("y", "x", "mp"), axis=0, tiled=True)
-    )[:, 0]
     part = w_merge.shape[0] // 2
     wm = lax.all_gather(
         lax.dynamic_slice_in_dim(w_merge, section * part, part, 0), "y", axis=0, tiled=False
@@ -602,15 +652,10 @@
     w_half = jnp.where(section == 0, w_mine[: FB // 2], swapped)
     w_first = lax.all_gather(w_half, "y", axis=0, tiled=False)
 
-    count = target.shape[0]
-    order = jnp.arange(count, dtype=jnp.int32)
-    position = jnp.sum(
-        ((target[:, None] == target[None, :]) & (order[:, None] > order[None, :])).astype(jnp.int32),
-        axis=1,
-    )
-    lslot = (target - y * SIDE) * TOK + position
-    gslot = jnp.where(target % SIDE == x, (target // SIDE) * TOK + position, -1)
-    gslot = lax.dynamic_slice_in_dim(gslot, y * 256, 256, 0)
+    z = lax.axis_index("mp")
+    place = jnp.arange(1024, dtype=jnp.int32)
+    repeated = jnp.broadcast_to(routes[:, 0][None, :], (64, 16)).reshape(1024)
+    placed = jnp.where(place // 16 == (y * SIDE + x) * SIDE + z, repeated, 0)[None, :]
 
     merged = vision_rows(patches, image_units[0], v_gain, v_qkv, v_out, merge_gain)
     pieces = merged.reshape(16, MERGE, SIDE, 320).transpose(2, 0, 1, 3).reshape(SIDE, 16, VD)
@@ -618,8 +663,8 @@
     at = jnp.arange(TOK, dtype=jnp.int32)
     mask = ((seq[:, None] == seq[None, :]) & (at[:, None] >= at[None, :])).astype(F32)
 
-    hidden = merge_call(pieces, wm, text, lslot[None, :])
-    return layers_call(hidden, w_first, w_mine, mask, gslot[:, None], row_grads)
+    hidden, gslot = merge_call(pieces, wm, text, placed)
+    return layers_call(hidden, w_first, w_mine, mask, gslot, row_grads)
 
 
 def solution(mesh):

time: 445 us -> 272 us (0.61)
  blocking collectives: 191 us -> 0 us
  Pallas kernels: 188 us -> 207 us
    all_gather x1 -> x0, blocking collectives: 191 us -> none  [shards(): lax.all_gather(sent, ('y', 'x', 'mp'), axis=0, tiled=True)]
    pallas_call x1, Pallas kernels: 40.3 us -> 63.3 us  [merge_call(): pl.pallas_call(merge_kernel, out_shape=(jax.ShapeDtypeStruct((2, SIDE * H...]
  transfers between devices with their start and end apart: 3 -> 3, of which waited for: 1 -> 1; matrix products, arithmetic and copies ran while one was open for 9% -> 14% of each run, Pallas kernels for 9% -> 23%
where the time goes in v3:
time: 272 us; the launch traced here: 270 us
  Pallas kernels  207 us (76%)
  local copies, waits for them, and re-layouts  21.1 us (8%)
  between operations  14.2 us (5%)
  other arithmetic  12 us (4%)
  matrix products  11.3 us (4%)
    pallas_call x1, Pallas kernels, layers_call(): pl.pallas_call(layers_kernel, out_shape=(jax.ShapeDtypeStruct((TOK, SIDE...  144 us
    pallas_call x1, Pallas kernels, merge_call(): pl.pallas_call(merge_kernel, out_shape=(jax.ShapeDtypeStruct((2, SIDE * H...  63.3 us
    dot_general x1, matrix products, vision_rows(): projected = jnp.dot(v_normed, v_qkv, preferred_element_type=F32).astype(BF)  6.89 us
    unnamed x22, local copies, waits for them, and re-layouts  5.46 us
  transfers between devices with their start and end apart: 3, of which 1 were waited for; matrix products, arithmetic and copies ran while one was open for 14% of the time, Pallas kernels for 23%

profile of v3, /device:TPU:0, one launch (start us, length us, event | category | flops | bytes accessed | tf_op | source)
XLA Modules:
  0.0 270.1 jit_solution(12055212845855076399)
XLA Ops:
  7.2 2.1 constant_dynamic-slice_fusion.1
  9.5 0.8 constant_dynamic-slice_fusion
  10.2 1.6 fusion.1
  11.9 1.1 copy-done.1
  12.9 1.2 fusion.9
  14.1 2.3 collective-permute-start
  16.5 1.7 collective-permute-done
  18.2 2.5 fusion.8
  21.1 6.9 %convolution_convert_fusion = bf16[64,3840]{1,0:T(8,128)(2,1)} fusion(bf16[1280,3840]{1,0:T(8,128)(2,1)} %param.17, bf16[64,1280]{1,0:T(8,128)(2,1)S(1)} %copy-done.3, f32[1280]{0:T(1024)S(1)} %copy-done.4, f32[64]{0:T(128)S(1)} %add_rsqrt_fusion.1, f32[64]{0:T(128)S(1)} %broadcast_multiply_fusion.1), kind=kOutput, calls=%fused_computation.1 | convolution fusion | flops 629800960 | bytes 10491392 | tf_op jit(solution)/shard_map/dot_general | solution.py:54
  28.0 3.0 %reshape.181 = bf16[64,3,16,80]{3,2,1,0:T(8,128)(2,1)} reshape(bf16[64,3840]{1,0:T(8,128)(2,1)} %convolution_convert_fusion) | data formatting | bytes 983040 | tf_op jit(solution)/shard_map/reshape | solution.py:55
  31.6 2.0 fusion.24
  33.8 0.8 copy-done.9
  34.8 2.4 fusion.10
  37.2 1.8 copy.31
  39.0 1.9 reshape.184
  40.9 1.7 fusion.26
  42.9 0.8 multiply_convert_fusion
  43.7 1.1 reshape_reshape.3
  45.6 1.8 reshape.185.pieces
  49.1 3.3 %pad_maximum_fusion.w_mine = bf16[512,2304]{1,0:T(8,128)(2,1)} fusion(bf16[512,1024]{1,0:T(8,128)(2,1)} %bitcast.32, bf16[512,1280]{1,0:T(8,128)(2,1)} %copy-done.1), kind=kLoop, calls=%fused_computation.4 | loop fusion | flops 4718592 | bytes 4718592 | tf_op jit(solution)/shard_map/concatenate | solution.py:650
  52.4 63.3 %merge.1 = (bf16[2,256,512]{2,1,0:T(8,128)(2,1)}, s32[256,128]{1,0:T(8,128)}) custom-call(bf16[4,16,1280]{2,1,0:T(8,128)(2,1)} %reshape.185.pieces, bf16[4,160,2048]{2,1,0:T(8,128)(2,1)} %bitcast.35, bf16[128,2048]{1,0:T(8,128)(2,1)} %text.1, s32[1,1024]{1,0:T(1,128)} %compare_select_fusion.placed), custom_call_target="tpu_custom_call" | custom-call | tf_op jit(solution)/shard_map/merge/pallas_call | solution.py:257
  115.7 144.0 %layers.1 = (bf16[128,2048]{1,0:T(8,128)(2,1)}, bf16[16,8192]{1,0:T(8,128)(2,1)}) custom-call(bf16[2,256,512]{2,1,0:T(8,128)(2,1)} %get-tuple-element.4.h, bf16[4,256,2304]{2,1,0:T(8,128)(2,1)} %bitcast.34, bf16[512,2304]{1,0:T(8,128)(2,1)} %pad_maximum_fusion.w_mine, f32[128,128]{1,0:T(8,128)} %fusion.22.mask, s32[256,128]{1,0:T(8,128)} %get-tuple-element.5.gslot, ...), custom_call_target="tpu_custom_call" | custom-call | tf_op jit(solution)/shard_map/layers/pallas_call | solution.py:579
  259.7 1.9 copy.47
  261.6 1.7 copy.48
  (45 shorter events, 4.1 us)
Async XLA Ops:
  7.2 33.8 %copy-start = (bf16[1280,1280]{1,0:T(8,128)(2,1)S(1)}, bf16[1280,1280]{1,0:T(8,128)(2,1)}, u32[]{:S(2)}) copy-start(bf16[1280,1280]{1,0:T(8,128)(2,1)} %param.18) | copy-start | bytes 9830404
  7.2 45.2 %all-gather.5.cloned.1.call-start = ((), (), s32[]{:S(2)}) async-start(), calls=%async_computation | async-start | bytes 3276800 | tf_op jit(solution)/shard_map/all_gather | solution.py:645
  9.4 106.3 %all-gather.7.cloned.1.call-start = ((), (), s32[]{:S(2)}) async-start(), calls=%async_computation.1 | async-start | bytes 5898240 | tf_op jit(solution)/shard_map/all_gather | solution.py:653
  9.5 3.5 %copy-start.2 = (bf16[1,512,1024]{2,1,0:T(8,128)(2,1)S(1)}, bf16[1,512,1024]{2,1,0:T(8,128)(2,1)}, u32[]{:S(2)}) copy-start(bf16[1,512,1024]{2,1,0:T(8,128)(2,1)} %param.26) | copy-start | bytes 3145732
  11.8 1.1 copy-start.1
  14.1 4.1 %collective-permute-start = (bf16[256,2304]{1,0:T(8,128)(2,1)}, bf16[256,2304]{1,0:T(8,128)(2,1)}, u32[]{:S(2)}, u32[]{:S(2)}) collective-permute-start(bf16[256,2304]{1,0:T(8,128)(2,1)} %fusion.9), channel_id=1, source_target_pairs={{0,64},{1,65},{2,66},{3,67},{4,68},{5,69},{6,70},{7,71},{8,72},{9,... | collective-permute-start | bytes 3538952 | tf_op jit(solution)/shard_map/ppermute | solution.py:651
  16.5 4.3 %copy-start.3 = (bf16[64,1280]{1,0:T(8,128)(2,1)S(1)}, bf16[64,1280]{1,0:T(8,128)(2,1)}, u32[]{:S(2)}) copy-start(bf16[64,1280]{1,0:T(8,128)(2,1)} %param.14) | copy-start | bytes 491524
  16.5 4.7 %copy-start.4 = (f32[1280]{0:T(1024)S(1)}, f32[1280]{0:T(1024)}, u32[]{:S(2)}) copy-start(f32[1280]{0:T(1024)} %param.16) | copy-start | bytes 15364
  21.1 10.0 %copy-start.7 = (s32[1,3]{1,0:T(1,128)S(1)}, s32[1,3]{1,0:T(1,128)}, u32[]{:S(2)}) copy-start(s32[1,3]{1,0:T(1,128)} %param.15) | copy-start | bytes 40
  33.8 0.8 copy-start.9
  39.0 3.9 %copy-start.5 = (f32[1280]{0:T(1024)S(1)}, f32[1280]{0:T(1024)}, u32[]{:S(2)}) copy-start(f32[1280]{0:T(1024)} %param.19) | copy-start | bytes 15364
  40.9 6.5 %copy-start.6 = (s32[16,1]{0,1:T(1,128)S(1)}, s32[16,1]{0,1:T(1,128)}, u32[]{:S(2)}) copy-start(s32[16,1]{0,1:T(1,128)} %param.21) | copy-start | bytes 196
  40.9 6.6 %copy-start.8 = (s32[1,3]{1,0:T(1,128)S(1)}, s32[1,3]{1,0:T(1,128)}, u32[]{:S(2)}) copy-start(s32[1,3]{1,0:T(1,128)} %param.23) | copy-start | bytes 40
Sparse Core Ops, SparseCore 0:
  9.7 37.7 all-gather.4
  49.1 62.6 all-gather.6

commit v4 on v3

--- a/solution.py
+++ b/solution.py
@@ -294,9 +294,9 @@
 def layers_kernel(
     h, w_first, w_mine, mask, gslot, grads,
     out, mg,
-    w, zbuf, acc, squares, kv, psend, rbuf, abuf, osend, orec, obuf,
+    w, zbuf, acc, squares, kv, psend, rbuf, abuf, osend, orec, orel, obuf,
     gbuf, gsend, grec, gz, mz,
-    w_sem, s_w0, r_w0, s_w1, r_w1, s_w2, r_w2,
+    w_sem, s_w0, r_w0, s_w1, r_w1, s_w2, r_w2, s_v1, r_v1, s_v2, r_v2,
     s_z, r_z, s_x, r_x, s_a, r_a, s_o, r_o, s_e, r_e,
     s_g, r_g, s_gx, r_gx, s_gz, r_gz,
 ):
@@ -310,9 +310,16 @@
     width = grads.shape[1]
     mine = pl.ds(pl.multiple_of(section * half, half), half)
 
-    own_load = pltpu.make_async_copy(w_first, w.at[0, :, mine, :], w_sem.at[0])
+    left = slice(0, rows // 2)
+    right = slice(rows // 2, rows)
+    first_cols = pl.ds(0, PW)
+    last_cols = pl.ds(PW, QW)
+    own_load = pltpu.make_async_copy(w_first, w.at[0, :, mine, first_cols], w_sem.at[0])
     own_load.start()
     own_shard = pltpu.make_async_copy(w_mine, w.at[1, y], w_sem.at[1])
+    own_out = pltpu.make_async_copy(
+        w_mine.at[:, last_cols], w.at[0, y, :, last_cols], w_sem.at[2]
+    )
     for part in range(2):
         zbuf[0, part, z] = h[part]
     greet(
@@ -322,7 +329,7 @@
         + [twin]
     )
 
-    z_copies, x_copies, a_copies, o_copies, e_copies = {}, {}, {}, {}, []
+    z_copies, f_copies, x_copies, a_copies, o_copies, e_copies = {}, {}, {}, {}, {}, []
 
     def spread(layer, part):
         z_copies[layer, part] = {
@@ -330,32 +337,57 @@
                 zbuf.at[layer, part, z], zbuf.at[layer, part, z],
                 s_z.at[layer, part, dz], r_z.at[layer, part, dz], {"mp": along(z, dz)},
             )
-            for dz in STEPS
+            for dz in (1, 3)
         }
 
+    def times(layer, part, dz):
+        zs = behind(z, dz)
+        wide = zbuf[layer, part, zs].astype(F32)
+        squared = jnp.sum(wide * wide, axis=1, keepdims=True)
+        if dz:
+            squares[part] += jnp.broadcast_to(squared, (rows, HD))
+        else:
+            squares[part] = jnp.broadcast_to(squared, (rows, HD))
+
+        @pl.loop(0, PW // 256)
+        def _(tile):
+            cols = pl.ds(pl.multiple_of(tile * 256, 256), 256)
+            product = jnp.dot(
+                zbuf[layer, part, zs], w[layer, zs, :, cols], preferred_element_type=F32
+            )
+            if dz:
+                acc[part, :, cols] += product
+            else:
+                acc[part, :, cols] = product
+
+    def passed(layer, part):
+        copies = z_copies[layer, part]
+        copies[1].wait()
+        zs = behind(z, 1)
+        f_copies[layer, part] = [
+            push(
+                zbuf.at[layer, part, zs, left], zbuf.at[layer, part, zs, left],
+                s_z.at[layer, part, 0], r_z.at[layer, part, 0], {"mp": along(z, 1)},
+            )
+        ]
+        copies[3].wait()
+        zs = along(z, 1)
+        f_copies[layer, part].append(
+            push(
+                zbuf.at[layer, part, zs, right], zbuf.at[layer, part, zs, right],
+                s_z.at[layer, part, 2], r_z.at[layer, part, 2], {"mp": along(z, 3)},
+            )
+        )
+
+    def own_part(layer, part):
+        times(layer, part, 0)
+
     def project(layer, part):
-        for dz in (0, 1, 3, 2):
-            zs = behind(z, dz)
-            if dz:
-                z_copies[layer, part][dz].wait()
-            wide = zbuf[layer, part, zs].astype(F32)
-            squared = jnp.sum(wide * wide, axis=1, keepdims=True)
-            if dz:
-                squares[part] += jnp.broadcast_to(squared, (rows, HD))
-            else:
-                squares[part] = jnp.broadcast_to(squared, (rows, HD))
-
-            @pl.loop(0, PW // 256)
-            def _(tile):
-                cols = pl.ds(pl.multiple_of(tile * 256, 256), 256)
-                product = jnp.dot(
-                    zbuf[layer, part, zs], w[layer, zs, :, cols], preferred_element_type=F32
-                )
-                if dz:
-                    acc[part, :, cols] += product
-                else:
-                    acc[part, :, cols] = product
-
+        times(layer, part, 1)
+        times(layer, part, 3)
+        for copy in f_copies[layer, part]:
+            copy.wait()
+        times(layer, part, 2)
         lane = lax.broadcasted_iota(jnp.int32, (HALF, HD), 1)
         copies = []
         for dx in STEPS:
@@ -417,8 +449,15 @@
     def output(layer, part):
         for copy in a_copies[layer, part]:
             copy.wait()
-        copies = []
-        for dz in (1, 3, 2, 0):
+        copies = {}
+
+        def send(name, src, dst, dz):
+            copies[name] = push(
+                src, dst, s_o.at[layer, part, name], r_o.at[layer, part, name],
+                {"mp": along(z, dz)},
+            )
+
+        for dz in (2, 1, 3, 0):
             zt = along(z, dz)
 
             @pl.loop(0, FB // 256)
@@ -429,21 +468,35 @@
                     (((1,), (1,)), ((), ())), preferred_element_type=F32,
                 ).astype(BF)
 
-            if dz:
-                copies.append(
-                    push(
-                        osend.at[layer, part, dz], orec.at[layer, part, dz],
-                        s_o.at[layer, part, dz], r_o.at[layer, part, dz], {"mp": zt},
-                    )
-                )
-        o_copies[layer, part] = copies
+            if dz == 2:
+                send(0, osend.at[layer, part, 2, left], orel.at[layer, part, 0], 1)
+                send(1, osend.at[layer, part, 2, right], orel.at[layer, part, 1], 3)
+            elif dz == 1:
+                send(2, osend.at[layer, part, 1, right], orec.at[layer, part, 0, right], 1)
+            elif dz == 3:
+                send(3, osend.at[layer, part, 3, left], orec.at[layer, part, 1, left], 3)
+        o_copies[layer, part] = copies, send
+
+    def relay(layer, part):
+        copies, send = o_copies[layer, part]
+        copies[0].wait()
+        osend[layer, part, 1, left] = (
+            osend[layer, part, 1, left].astype(F32) + orel[layer, part, 0].astype(F32)
+        ).astype(BF)
+        send(4, osend.at[layer, part, 1, left], orec.at[layer, part, 0, left], 1)
+        copies[1].wait()
+        osend[layer, part, 3, right] = (
+            osend[layer, part, 3, right].astype(F32) + orel[layer, part, 1].astype(F32)
+        ).astype(BF)
+        send(5, osend.at[layer, part, 3, right], orec.at[layer, part, 1, right], 3)
 
     def finish(layer, part):
         update = osend[layer, part, 0].astype(F32)
-        for copy in o_copies[layer, part]:
-            copy.wait()
-        for dz in STEPS:
-            update = update + orec[layer, part, dz].astype(F32)
+        copies, _ = o_copies[layer, part]
+        for name in (2, 3, 4, 5):
+            copies[name].wait()
+        for side in range(2):
+            update = update + orec[layer, part, side].astype(F32)
         fresh = (zbuf[layer, part, z].astype(F32) + update).astype(BF)
         if layer == 0:
             zbuf[1, part, z] = fresh
@@ -463,8 +516,7 @@
         ]
 
     spread(0, 0)
-    spread(0, 1)
-    twin_copy = push(w_first, w.at[0, :, mine, :], s_w0.at[0], r_w0.at[0], twin)
+    twin_copy = push(w_first, w.at[0, :, mine, first_cols], s_w0.at[0], r_w0.at[0], twin)
 
     def shard_copy(dy):
         return pltpu.make_async_remote_copy(
@@ -479,80 +531,150 @@
             recv_sem=r_w2.at[dy], device_id=twin, device_id_type=pl.DeviceIdType.MESH,
         )
 
-    @pl.when(section == 1)
+    def out_copy(dy):
+        return pltpu.make_async_remote_copy(
+            src_ref=w_mine.at[:, last_cols], dst_ref=w.at[0, y, :, last_cols],
+            send_sem=s_v1.at[dy], recv_sem=r_v1.at[dy],
+            device_id={"y": along(y, dy)}, device_id_type=pl.DeviceIdType.MESH,
+        )
+
+    def out_forward(dy):
+        ys = behind(y, dy)
+        return pltpu.make_async_remote_copy(
+            src_ref=w.at[0, ys, :, last_cols], dst_ref=w.at[0, ys, :, last_cols],
+            send_sem=s_v2.at[dy], recv_sem=r_v2.at[dy], device_id=twin,
+            device_id_type=pl.DeviceIdType.MESH,
+        )
+
+    @pl.when(section == 0)
     def _():
         for dy in STEPS:
-            shard_copy(dy).start()
-        own_shard.start()
-
-    own_load.wait()
-    twin_copy.wait()
-    project(0, 0)
-    project(0, 1)
-    attend(0, 0)
-    attend(0, 1)
-    g_copies = [
-        push(grads, gbuf.at[y], s_g.at[dy], r_g.at[dy], {"y": along(y, dy)}) for dy in STEPS
-    ]
-    gbuf[y] = grads[...]
-    output(0, 0)
-    output(0, 1)
-
-    @pl.when(section == 1)
-    def _():
-        own_shard.wait()
-        forward_copy(0).start()
+            out_copy(dy).start()
+        own_out.start()
+
+    def start_last(layer, part):
+        @pl.when(section == 1)
+        def _():
+            for dy in STEPS:
+                shard_copy(dy).start()
+            own_shard.start()
+
+    def share_out(layer, part):
+        @pl.when(section == 0)
+        def _():
+            own_out.wait()
+            out_forward(0).start()
+            for dy in STEPS:
+                out_copy(dy).wait()
+                out_forward(dy).start()
+
+        @pl.when(section == 1)
+        def _():
+            for dy in range(SIDE):
+                out_forward(dy).wait_recv()
+
+    g_copies, gx_copies, gz_copies = [], [], []
+
+    def ready(layer, part):
+        if layer == 0:
+            own_load.wait()
+            twin_copy.wait()
+            return
+
+        @pl.when(section == 0)
+        def _():
+            for dy in range(SIDE):
+                forward_copy(dy).wait_recv()
+
+    def forward(layer, part):
+        @pl.when(section == 1)
+        def _():
+            own_shard.wait()
+            forward_copy(0).start()
+            for dy in STEPS:
+                shard_copy(dy).wait()
+                forward_copy(dy).start()
+
+    def give(layer, part):
+        gbuf[y] = grads[...]
         for dy in STEPS:
-            shard_copy(dy).wait()
-            forward_copy(dy).start()
-
-    finish(0, 0)
-    spread(1, 0)
-    finish(0, 1)
-    spread(1, 1)
-
-    @pl.when(section == 0)
-    def _():
-        for dy in range(SIDE):
-            forward_copy(dy).wait_recv()
-
-    project(1, 0)
-    project(1, 1)
-    attend(1, 0)
-    attend(1, 1)
-
-    for copy in g_copies:
-        copy.wait()
-    gx_copies = []
-    for dx in (1, 3, 2, 0):
-        xt = along(x, dx)
-        wanted = gslot[pl.ds(pl.multiple_of(xt * 64, 64), 64), :1]
-        lanes = lax.broadcasted_iota(jnp.int32, (64, SIDE * TOK), 1)
-        chosen = jnp.where(lanes == wanted, 1.0, 0.0).astype(BF)
-        gsend[dx] = jnp.dot(
-            chosen, gbuf[...].reshape(SIDE * TOK, width), preferred_element_type=F32
-        ).astype(BF)
-        if dx:
-            gx_copies.append(
-                push(gsend.at[dx], grec.at[dx], s_gx.at[dx], r_gx.at[dx], {"x": xt})
-            )
-
-    output(1, 0)
-    output(1, 1)
-    for copy in gx_copies:
-        copy.wait()
-    found = gsend[0].astype(F32)
-    for dx in STEPS:
-        found = found + grec[dx].astype(F32)
-    gz[...] = found.astype(BF).reshape(SIDE, 16, width)
-    gz_copies = []
-    for dz in STEPS:
-        zt = along(z, dz)
-        gz_copies.append(push(gz.at[zt], mz.at[z], s_gz.at[dz], r_gz.at[dz], {"mp": zt}))
-    mz[z] = gz[z]
-
-    finish(1, 0)
-    finish(1, 1)
+            g_copies.append(
+                push(grads, gbuf.at[y], s_g.at[dy], r_g.at[dy], {"y": along(y, dy)})
+            )
+
+    def choose(layer, part):
+        for copy in g_copies:
+            copy.wait()
+        for dx in (1, 3, 2, 0):
+            xt = along(x, dx)
+            wanted = gslot[pl.ds(pl.multiple_of(xt * 64, 64), 64), :1]
+            lanes = lax.broadcasted_iota(jnp.int32, (64, SIDE * TOK), 1)
+            chosen = jnp.where(lanes == wanted, 1.0, 0.0).astype(BF)
+            gsend[dx] = jnp.dot(
+                chosen, gbuf[...].reshape(SIDE * TOK, width), preferred_element_type=F32
+            ).astype(BF)
+            if dx:
+                gx_copies.append(
+                    push(gsend.at[dx], grec.at[dx], s_gx.at[dx], r_gx.at[dx], {"x": xt})
+                )
+
+    def hand(layer, part):
+        for copy in gx_copies:
+            copy.wait()
+        found = gsend[0].astype(F32)
+        for dx in STEPS:
+            found = found + grec[dx].astype(F32)
+        gz[...] = found.astype(BF).reshape(SIDE, 16, width)
+        for dz in STEPS:
+            zt = along(z, dz)
+            gz_copies.append(
+                push(gz.at[zt], mz.at[z], s_gz.at[dz], r_gz.at[dz], {"mp": zt})
+            )
+        mz[z] = gz[z]
+
+    for stage, layer, part in (
+        (ready, 0, 0),
+        (own_part, 0, 0),
+        (passed, 0, 0),
+        (spread, 0, 1),
+        (project, 0, 0),
+        (own_part, 0, 1),
+        (attend, 0, 0),
+        (start_last, 0, 0),
+        (passed, 0, 1),
+        (project, 0, 1),
+        (share_out, 0, 0),
+        (output, 0, 0),
+        (attend, 0, 1),
+        (relay, 0, 0),
+        (output, 0, 1),
+        (finish, 0, 0),
+        (spread, 1, 0),
+        (relay, 0, 1),
+        (forward, 0, 0),
+        (ready, 1, 0),
+        (own_part, 1, 0),
+        (give, 0, 0),
+        (finish, 0, 1),
+        (passed, 1, 0),
+        (spread, 1, 1),
+        (project, 1, 0),
+        (own_part, 1, 1),
+        (attend, 1, 0),
+        (passed, 1, 1),
+        (project, 1, 1),
+        (output, 1, 0),
+        (attend, 1, 1),
+        (relay, 1, 0),
+        (output, 1, 1),
+        (choose, 1, 0),
+        (finish, 1, 0),
+        (relay, 1, 1),
+        (hand, 1, 0),
+        (finish, 1, 1),
+    ):
+        stage(layer, part)
+
     for copy in gz_copies:
         copy.wait()
     for block in range(SIDE):
@@ -567,6 +689,11 @@
     def _():
         for dy in range(SIDE):
             forward_copy(dy).wait_send()
+
+    @pl.when(section == 0)
+    def _():
+        for dy in range(SIDE):
+            out_forward(dy).wait_send()
 
 
 def layers_call(h, w_first, w_mine, mask, gslot, grads):
@@ -594,21 +721,24 @@
             pltpu.VMEM((2, 2, SIDE, HALF, PT), BF),
             pltpu.VMEM((2, 2, SIDE, HALF, QW), BF),
             pltpu.VMEM((2, 2, SIDE, rows, FB), BF),
-            pltpu.VMEM((2, 2, SIDE, rows, FB), BF),
+            pltpu.VMEM((2, 2, 2, rows, FB), BF),
+            pltpu.VMEM((2, 2, 2, rows // 2, FB), BF),
             pltpu.VMEM((SIDE, 2, HALF, FB), BF),
             pltpu.VMEM((SIDE, TOK, width), BF),
             pltpu.VMEM((SIDE, 64, width), BF),
             pltpu.VMEM((SIDE, 64, width), BF),
             pltpu.VMEM((SIDE, 16, width), BF),
             pltpu.VMEM((SIDE, 16, width), BF),
-            dma((2,)),
+            dma((3,)),
             dma((1,)), dma((1,)),
+            dma((SIDE,)), dma((SIDE,)),
+            dma((SIDE,)), dma((SIDE,)),
             dma((SIDE,)), dma((SIDE,)),
             dma((SIDE,)), dma((SIDE,)),
             stage, stage,
             stage, stage,
             stage, stage,
-            stage, stage,
+            dma((2, 2, 6)), dma((2, 2, 6)),
             dma((2, SIDE)), dma((2, SIDE)),
             dma((SIDE,)), dma((SIDE,)),
             dma((SIDE,)), dma((SIDE,)),
@@ -648,8 +778,8 @@
     gain = lax.dynamic_slice_in_dim(lang_gain[0], (y * SIDE + x) * FB, FB, 0)
     scaled = (w_qkv[0].astype(F32) * gain[:, None]).astype(BF)
     w_mine = jnp.concatenate([scaled, wo_t[0]], axis=1)
-    swapped = lax.ppermute(w_mine[FB // 2 :], "section", [(0, 1)])
-    w_half = jnp.where(section == 0, w_mine[: FB // 2], swapped)
+    swapped = lax.ppermute(scaled[FB // 2 :], "section", [(0, 1)])
+    w_half = jnp.where(section == 0, scaled[: FB // 2], swapped)
     w_first = lax.all_gather(w_half, "y", axis=0, tiled=False)
 
     z = lax.axis_index("mp")

time: 272 us -> 271 us (level)
    pallas_call x1, Pallas kernels: 144 us -> 156 us  [layers_call(): pl.pallas_call(layers_kernel, out_shape=(jax.ShapeDtypeStruct((TOK, SIDE...]
    pallas_call x1, Pallas kernels: 63.3 us -> 53.3 us  [merge_call(): pl.pallas_call(merge_kernel, out_shape=(jax.ShapeDtypeStruct((2, SIDE * H...]
    unnamed x22 -> x20, local copies, waits for them, and re-layouts: 5.46 us -> 5.52 us
  transfers between devices with their start and end apart: 3 -> 3, of which waited for: 1 -> 1; matrix products, arithmetic and copies ran while one was open for 14% -> 13% of each run, Pallas kernels for 23% -> 20%
where the time goes in v4:
time: 271 us; the launch traced here: 270 us
  Pallas kernels  209 us (77%)
  local copies, waits for them, and re-layouts  22.1 us (8%)
  between operations  14.2 us (5%)
  matrix products  11.4 us (4%)
  other arithmetic  10.2 us (4%)
    pallas_call x1, Pallas kernels, layers_call(): pl.pallas_call(layers_kernel, out_shape=(jax.ShapeDtypeStruct((TOK, SIDE...  156 us
    pallas_call x1, Pallas kernels, merge_call(): pl.pallas_call(merge_kernel, out_shape=(jax.ShapeDtypeStruct((2, SIDE * H...  53.3 us
    dot_general x1, matrix products, vision_rows(): projected = jnp.dot(v_normed, v_qkv, preferred_element_type=F32).astype(BF)  6.94 us
    unnamed x20, local copies, waits for them, and re-layouts  5.52 us
  transfers between devices with their start and end apart: 3, of which 1 were waited for; matrix products, arithmetic and copies ran while one was open for 13% of the time, Pallas kernels for 20%

profile of v4, /device:TPU:0, one launch (start us, length us, event | category | flops | bytes accessed | tf_op | source)
XLA Modules:
  0.0 270.2 jit_solution(12936103623743460247)
XLA Ops:
  7.2 2.2 constant_dynamic-slice_fusion.1
  10.2 1.6 fusion.1
  11.8 1.1 copy-done.1
  13.0 0.9 slice.24
  13.9 2.1 collective-permute-start
  16.3 0.8 collective-permute-done
  17.2 2.0 slice_select_fusion
  19.2 6.9 %convolution_convert_fusion = bf16[64,3840]{1,0:T(8,128)(2,1)} fusion(bf16[1280,3840]{1,0:T(8,128)(2,1)} %param.17, bf16[64,1280]{1,0:T(8,128)(2,1)S(1)} %copy-done.2, f32[1280]{0:T(1024)S(1)} %copy-done.3, f32[64]{0:T(128)S(1)} %add_rsqrt_fusion.1, f32[64]{0:T(128)S(1)} %broadcast_multiply_fusion.1), kind=kOutput, calls=%fused_computation.1 | convolution fusion | flops 629800960 | bytes 10491392 | tf_op jit(solution)/shard_map/dot_general | solution.py:54
  26.2 3.1 %reshape.181 = bf16[64,3,16,80]{3,2,1,0:T(8,128)(2,1)} reshape(bf16[64,3840]{1,0:T(8,128)(2,1)} %convolution_convert_fusion) | data formatting | bytes 983040 | tf_op jit(solution)/shard_map/reshape | solution.py:55
  29.8 2.0 fusion.21
  32.0 0.8 copy-done.8
  33.0 2.4 fusion.7
  35.4 1.8 copy.31
  37.2 1.9 reshape.184
  39.1 1.7 fusion.23
  41.1 0.8 multiply_convert_fusion
  41.9 1.1 reshape_reshape.3
  43.1 0.8 copy.44
  43.8 1.8 reshape.185.pieces
  47.3 3.2 %pad_maximum_fusion.w_mine = bf16[512,2304]{1,0:T(8,128)(2,1)} fusion(bf16[512,1024]{1,0:T(8,128)(2,1)} %bitcast.33, bf16[512,1280]{1,0:T(8,128)(2,1)} %copy-done.1), kind=kLoop, calls=%fused_computation.5 | loop fusion | flops 4718592 | bytes 4718592 | tf_op jit(solution)/shard_map/concatenate | solution.py:780
  50.6 53.3 %merge.1 = (bf16[2,256,512]{2,1,0:T(8,128)(2,1)}, s32[256,128]{1,0:T(8,128)}) custom-call(bf16[4,16,1280]{2,1,0:T(8,128)(2,1)} %reshape.185.pieces, bf16[4,160,2048]{2,1,0:T(8,128)(2,1)} %bitcast.31, bf16[128,2048]{1,0:T(8,128)(2,1)} %text.1, s32[1,1024]{1,0:T(1,128)} %compare_select_fusion.placed), custom_call_target="tpu_custom_call" | custom-call | tf_op jit(solution)/shard_map/merge/pallas_call | solution.py:257
  103.9 155.9 %layers.1 = (bf16[128,2048]{1,0:T(8,128)(2,1)}, bf16[16,8192]{1,0:T(8,128)(2,1)}) custom-call(bf16[2,256,512]{2,1,0:T(8,128)(2,1)} %get-tuple-element.4.h, bf16[4,256,1280]{2,1,0:T(8,128)(2,1)} %bitcast.32, bf16[512,2304]{1,0:T(8,128)(2,1)} %pad_maximum_fusion.w_mine, f32[128,128]{1,0:T(8,128)} %fusion.19.mask, s32[256,128]{1,0:T(8,128)} %get-tuple-element.5.gslot, ...), custom_call_target="tpu_custom_call" | custom-call | tf_op jit(solution)/shard_map/layers/pallas_call | solution.py:706
  259.8 1.9 copy.47
  261.7 1.7 copy.48
  (43 shorter events, 4.0 us)
Async XLA Ops:
  7.2 32.0 %copy-start = (bf16[1280,1280]{1,0:T(8,128)(2,1)S(1)}, bf16[1280,1280]{1,0:T(8,128)(2,1)}, u32[]{:S(2)}) copy-start(bf16[1280,1280]{1,0:T(8,128)(2,1)} %param.18) | copy-start | bytes 9830404
  7.2 43.4 %all-gather.5.cloned.1.call-start = ((), (), s32[]{:S(2)}) async-start(), calls=%async_computation | async-start | bytes 3276800 | tf_op jit(solution)/shard_map/all_gather | solution.py:775
  9.4 6.5 %copy-start.2 = (bf16[64,1280]{1,0:T(8,128)(2,1)S(1)}, bf16[64,1280]{1,0:T(8,128)(2,1)}, u32[]{:S(2)}) copy-start(bf16[64,1280]{1,0:T(8,128)(2,1)} %param.14) | copy-start | bytes 491524
  9.5 94.4 %all-gather.7.cloned.1.call-start = ((), (), s32[]{:S(2)}) async-start(), calls=%async_computation.1 | async-start | bytes 3276800 | tf_op jit(solution)/shard_map/all_gather | solution.py:783
  11.8 1.2 copy-start.1
  13.0 6.2 %copy-start.3 = (f32[1280]{0:T(1024)S(1)}, f32[1280]{0:T(1024)}, u32[]{:S(2)}) copy-start(f32[1280]{0:T(1024)} %param.16) | copy-start | bytes 15364
  13.9 3.3 %collective-permute-start = (bf16[256,1280]{1,0:T(8,128)(2,1)}, bf16[256,1280]{1,0:T(8,128)(2,1)}, u32[]{:S(2)}, u32[]{:S(2)}) collective-permute-start(bf16[256,1280]{1,0:T(8,128)(2,1)} %slice.24), channel_id=1, source_target_pairs={{0,64},{1,65},{2,66},{3,67},{4,68},{5,69},{6,70},{7,71},{8,72},{9,... | collective-permute-start | bytes 1966088 | tf_op jit(solution)/shard_map/ppermute | solution.py:781
  19.2 10.0 %copy-start.6 = (s32[1,3]{1,0:T(1,128)S(1)}, s32[1,3]{1,0:T(1,128)}, u32[]{:S(2)}) copy-start(s32[1,3]{1,0:T(1,128)} %param.15) | copy-start | bytes 40
  32.0 0.8 copy-start.8
  35.4 5.7 %copy-start.4 = (f32[1280]{0:T(1024)S(1)}, f32[1280]{0:T(1024)}, u32[]{:S(2)}) copy-start(f32[1280]{0:T(1024)} %param.19) | copy-start | bytes 15364
  39.1 6.5 %copy-start.5 = (s32[16,1]{0,1:T(1,128)S(1)}, s32[16,1]{0,1:T(1,128)}, u32[]{:S(2)}) copy-start(s32[16,1]{0,1:T(1,128)} %param.21) | copy-start | bytes 196
  39.1 6.6 %copy-start.7 = (s32[1,3]{1,0:T(1,128)S(1)}, s32[1,3]{1,0:T(1,128)}, u32[]{:S(2)}) copy-start(s32[1,3]{1,0:T(1,128)} %param.23) | copy-start | bytes 40
Sparse Core Ops, SparseCore 0:
  9.7 37.6 all-gather.4
  49.0 35.4 all-gather.6

commit v5 on v4

v5 whole, which is shorter than its diff:
```python
import functools
import math

import jax
import jax.numpy as jnp
from jax import lax
from jax.experimental import pallas as pl
from jax.experimental.pallas import tpu as pltpu
from jax.sharding import PartitionSpec as P

QH = 32
KVH = 4
HD = 128
VD = 1280
VH = 16
VHD = 80
SIDE = 4
TOK = 128
HALF = TOK // 2
STEPS = (1, 3, 2)
FB = 512
HEADS = QH // KVH
QW = HEADS * HD
PW = QW + 2 * HD
PT = PW + HD
D = 8192
PATCH = 64
UNITS = 16
PIECE = VD // SIDE
PADDED = 384
COUNT = 1024
TILE = 256
SLOTS = 6
EPSILON = 1e-06
VMEM_LIMIT = 62 * 1024 * 1024
BF = jnp.bfloat16
F32 = jnp.float32
MESH = pl.DeviceIdType.MESH


def layer_norm(values, norm_gain):
    centre = jnp.mean(values, axis=-1, keepdims=True)
    centred = values - centre
    variance = jnp.mean(centred * centred, axis=-1, keepdims=True)
    return centred * lax.rsqrt(variance + EPSILON) * norm_gain


def remote(src, dst, send_sem, recv_sem, where):
    return pltpu.make_async_remote_copy(
        src_ref=src, dst_ref=dst, send_sem=send_sem, recv_sem=recv_sem,
        device_id=where, device_id_type=MESH,
    )


def push(src, dst, send_sem, recv_sem, where):
    copy = remote(src, dst, send_sem, recv_sem, where)
    copy.start()
    return copy


def greet(partners):
    barrier = pltpu.get_barrier_semaphore()
    for where in partners:
        pl.semaphore_signal(barrier, inc=1, device_id=where, device_id_type=MESH)
    pl.semaphore_wait(barrier, len(partners))


def along(index, step):
    return lax.rem(index + step, SIDE)


def behind(index, step):
    return lax.rem(index + SIDE - step, SIDE)


def one_hot(condition):
    return jnp.where(condition, 1.0, 0.0).astype(BF)


def iota(shape, dimension):
    return lax.broadcasted_iota(jnp.int32, shape, dimension)


def segments(index, lengths):
    first = lengths[0, 0]
    second = first + lengths[0, 1]
    return jnp.where(index >= first, 1, 0) + jnp.where(index >= second, 1, 0)


def whole_kernel(
    patches, units, v_gain, v_qkv, v_out, merge_gain, w_merge, routes, text, lengths,
    lang_gain, w_qkv, wo_t, grads,
    out, mg,
    ring, wraw, wmv, w, v_proj, v_scores, v_weights, v_att, v_hidden, pieces, xbuf, part, msend, mrecv, ybuf, tbuf, pick,
    placed, rt, ry, tri, line, gslot,
    zbuf, acc, squares, kv, psend, rbuf, abuf, osend, orec, orel, obuf,
    gbuf, gsend, grec, gz, mz,
    v_sem, l_sem, s_w, r_w, s_rt, r_rt, s_ry, r_ry, s_pl, r_pl, s_mx, r_mx, s_my, r_my, s_t, r_t,
    s_z, r_z, s_x, r_x, s_a, r_a, s_o, r_o, s_e, r_e,
    s_g, r_g, s_gy, r_gy, s_gz, r_gz,
):
    section = lax.axis_index("section")
    x = lax.axis_index("x")
    y = lax.axis_index("y")
    z = lax.axis_index("mp")
    twin = {"section": 1 - section}
    rows = SIDE * HALF
    width = grads.shape[1]
    half = wmv.shape[2]
    plane = [(dx, dz) for dx in range(SIDE) for dz in range(SIDE) if dx or dz]
    left = slice(0, rows // 2)
    right = slice(rows // 2, rows)

    own_merge = pltpu.make_async_copy(
        w_merge.at[pl.ds(pl.multiple_of(section * half, half), half), :],
        wmv.at[y, section], l_sem.at[0],
    )
    own_merge.start()
    v_tiles = [
        pltpu.make_async_copy(
            (v_qkv if tile < 15 else v_out).at[:, pl.ds((tile if tile < 15 else tile - 15) * TILE, TILE)],
            ring.at[tile % SLOTS], v_sem.at[tile % SLOTS],
        )
        for tile in range(20)
    ]
    for tile in range(SLOTS):
        v_tiles[tile].start()
    raw_load = pltpu.make_async_copy(w_qkv.at[0], wraw, l_sem.at[1])
    raw_load.start()
    own_out = pltpu.make_async_copy(
        wo_t.at[0], w.at[section, y, :, pl.ds(PW, QW)], l_sem.at[2]
    )
    own_out.start()
    own_text = pltpu.make_async_copy(
        text.at[:, pl.ds(pl.multiple_of(x * FB, FB), FB)], tbuf.at[x], l_sem.at[3]
    )
    own_text.start()
    own_grads = pltpu.make_async_copy(grads, gbuf.at[x], l_sem.at[4])
    own_grads.start()

    lane = iota((1, COUNT), 1)
    base = ((y * SIDE + x) * SIDE + z) * UNITS
    row = jnp.zeros((1, COUNT), jnp.int32)
    for unit in range(UNITS):
        row = jnp.where(lane == base + unit, routes[unit, 0], row)
    placed[...] = row
    rt[x * SIDE + z] = row

    greet(
        [{"x": along(x, dx), "mp": along(z, dz)} for dx, dz in plane]
        + [{"y": along(y, dy)} for dy in STEPS]
        + [twin]
    )

    def shared(number, block, low, high):
        def own_copy(dy):
            return remote(
                block(y), block(y), s_w.at[number, dy], r_w.at[number, dy], {"y": along(y, dy)}
            )

        def up_copy():
            ref = low(behind(y, 1))
            return remote(ref, ref, s_w.at[number, 0], r_w.at[number, 0], {"y": along(y, 1)})

        def down_copy():
            ref = high(along(y, 1))
            return remote(ref, ref, s_w.at[number, 2], r_w.at[number, 2], {"y": along(y, 3)})

        def twin_copy(source):
            return remote(
                block(source), block(source), s_w.at[number, SIDE + source],
                r_w.at[number, SIDE + source], twin,
            )

        def begin():
            own_copy(1).start()
            own_copy(3).start()

        def middle():
            own_copy(1).wait()
            up_copy().start()
            own_copy(3).wait()
            down_copy().start()

        def end():
            up_copy().wait()
            down_copy().wait()
            for source in range(SIDE):
                twin_copy(source).start()

        def taken():
            for source in range(SIDE):
                twin_copy(source).wait_recv()

        def given():
            for source in range(SIDE):
                twin_copy(source).wait_send()

        return begin, middle, end, taken, given

    mid = wmv.shape[3] // 2
    merge_w = shared(
        0,
        lambda ys: wmv.at[ys, section],
        lambda ys: wmv.at[ys, section, :, pl.ds(0, mid)],
        lambda ys: wmv.at[ys, section, :, pl.ds(mid, mid)],
    )

    def layer_shard(number, layer, first, amount):
        cols = pl.ds(first, amount)
        return shared(
            number,
            lambda ys: w.at[layer, ys, :, cols],
            lambda ys: w.at[layer, ys, pl.ds(0, FB // 2), cols],
            lambda ys: w.at[layer, ys, pl.ds(FB // 2, FB // 2), cols],
        )

    qkv_w = layer_shard(1, 0, 0, PW)
    out_w = layer_shard(2, 0, PW, QW)
    last_w = layer_shard(3, 1, 0, PW + QW)

    def only(at, *actions):
        @pl.when(section == at)
        def _():
            for action in actions:
                action()

    own_merge.wait()
    merge_w[0]()
    route_copies = [
        push(
            placed, rt.at[x * SIDE + z], s_rt.at[dx * SIDE + dz], r_rt.at[dx * SIDE + dz],
            {"x": along(x, dx), "mp": along(z, dz)},
        )
        for dx, dz in plane
    ]
    text_copies = []
    for dx in STEPS:
        xt = along(x, dx)
        text_copies.append(
            push(
                text.at[:, pl.ds(pl.multiple_of(xt * FB, FB), FB)], tbuf.at[x],
                s_t.at[dx], r_t.at[dx], {"x": xt},
            )
        )
    grad_copies = [
        push(grads, gbuf.at[x], s_g.at[dx], r_g.at[dx], {"x": along(x, dx)}) for dx in STEPS
    ]

    order = iota((PATCH, PATCH), 0)
    swap = one_hot(iota((PATCH, PATCH), 1) == (order & 15) * SIDE + (order >> 4))
    patch = jnp.dot(swap, patches[...], preferred_element_type=F32)
    normed = layer_norm(patch, v_gain[...]).astype(BF)
    for tile in range(15):
        v_tiles[tile].wait()
        v_proj[:, tile * TILE : (tile + 1) * TILE] = jnp.dot(
            normed, ring[tile % SLOTS], preferred_element_type=F32
        ).astype(BF)
        if tile + SLOTS < 20:
            v_tiles[tile + SLOTS].start()

    windows = []
    for head in range(VH):
        start = min(head * VHD // 128 * 128, VD - 256)
        lanes = iota((PATCH, 256), 1) + start
        windows.append((start, (lanes >= head * VHD) & (lanes < (head + 1) * VHD)))
    for head, (start, inside) in enumerate(windows):
        query = v_proj[:, start : start + 256].astype(F32)
        query = jnp.where(inside, query, 0.0).astype(BF)
        key = v_proj[:, VD + start : VD + start + 256]
        v_scores[head * PATCH : (head + 1) * PATCH, :] = lax.dot_general(
            query, key, (((1,), (1,)), ((), ())), preferred_element_type=F32
        )
    image_q = segments(iota((VH * PATCH, PATCH), 0) & 15, units)
    image_k = segments(iota((VH * PATCH, PATCH), 1) & 15, units)
    scores = jnp.where(image_q == image_k, v_scores[...] / math.sqrt(VHD), -1e30)
    top = jnp.max(scores, axis=1, keepdims=True)
    weights = jnp.exp(scores - top)
    v_weights[...] = (weights / jnp.sum(weights, axis=1, keepdims=True)).astype(BF)
    v_att[...] = jnp.zeros((PATCH, VD), F32)
    for head, (start, inside) in enumerate(windows):
        mixed = jnp.dot(
            v_weights[head * PATCH : (head + 1) * PATCH, :],
            v_proj[:, 2 * VD + start : 2 * VD + start + 256],
            preferred_element_type=F32,
        )
        v_att[:, start : start + 256] += jnp.where(inside, mixed, 0.0)
    attended = v_att[...].astype(BF)
    for tile in range(5):
        v_tiles[15 + tile].wait()
        cols = slice(tile * TILE, (tile + 1) * TILE)
        v_hidden[:, cols] = (
            patch[:, cols]
            + jnp.dot(attended, ring[(15 + tile) % SLOTS], preferred_element_type=F32)
        ).astype(BF).astype(F32)
    merged = layer_norm(v_hidden[...], merge_gain[...])
    for block in range(SIDE):
        pieces[block, :, :, :PIECE] = merged[:, block * PIECE : (block + 1) * PIECE].astype(BF).reshape(
            SIDE, UNITS, PIECE
        )
        pieces[block, :, :, PIECE:] = jnp.zeros((SIDE, UNITS, PADDED - PIECE), BF)
    plane_copies = []
    for dx, dz in plane:
        xt = along(x, dx)
        plane_copies.append(
            push(
                pieces.at[xt], xbuf.at[x * SIDE + z],
                s_pl.at[dx * SIDE + dz], r_pl.at[dx * SIDE + dz],
                {"x": xt, "mp": along(z, dz)},
            )
        )
    xbuf[x * SIDE + z] = pieces[x]

    merge_w[1]()
    raw_load.wait()
    shard = y * SIDE + x
    gain = lang_gain[:, pl.ds(pl.multiple_of(shard * FB, FB), FB)]
    gain = jnp.transpose(jnp.broadcast_to(gain, (128, FB)))
    for tile in range(PW // 128):
        cols = slice(tile * 128, (tile + 1) * 128)
        w[section, y, :, cols] = (wraw[:, cols].astype(F32) * gain).astype(BF)
    own_out.wait()
    only(0, qkv_w[0])

    for block in range(SIDE):
        before = iota((256, COUNT), 0) + block * 256
        tri[block * 256 : (block + 1) * 256, :] = one_hot(before < iota((256, COUNT), 1))
    for copy in route_copies:
        copy.wait()
    known = rt[0]
    for source in range(1, SIDE * SIDE):
        known = known + rt[source]
    ry[y] = known
    ry_copies = [
        push(ry.at[y], ry.at[y], s_ry.at[dy], r_ry.at[dy], {"y": along(y, dy)})
        for dy in STEPS
    ]
    for copy in plane_copies:
        copy.wait()
    merge_w[2]()
    merge_w[3]()

    def product(dx):
        cols = pl.ds(pl.multiple_of(along(x, dx) * FB, FB), FB)
        total = None
        for patch_at in range(SIDE):
            piece = xbuf[:, patch_at].reshape(SIDE * SIDE * UNITS, PADDED)[:, :PIECE]
            weights = wmv[patch_at, :, :, cols].reshape(PIECE, FB)
            term = jnp.dot(piece, weights, preferred_element_type=F32)
            total = term if total is None else total + term
        return total

    m_copies = []
    for dx in STEPS:
        msend[dx] = product(dx).astype(BF)
        m_copies.append(
            push(msend.at[dx], mrecv.at[dx], s_mx.at[dx], r_mx.at[dx], {"x": along(x, dx)})
        )
    part[...] = product(0)

    for copy in ry_copies:
        copy.wait()
    target = ry[0] + ry[1] + ry[2] + ry[3]
    named = jnp.where(iota((16, COUNT), 0) == target, 1.0, 0.0)
    earlier = jnp.dot(named.astype(BF), tri[...], preferred_element_type=F32)
    position = jnp.sum(named * earlier, axis=0, keepdims=True).astype(jnp.int32)
    slots = (target - y * SIDE) * TOK + position
    for block in range(SIDE):
        wanted = iota((TOK, COUNT), 0) + block * TOK
        pick[block * TOK : (block + 1) * TOK, :] = one_hot(wanted == slots)
    line[...] = jnp.where((target >> 2) == y, (target & 3) * TOK + position + 1, 0)
    down = iota((256, COUNT), 0)
    chosen_rows = one_hot(iota((256, COUNT), 1) == (down >> 6) * 256 + x * 64 + (down & 63))

    def upright(values):
        wide = jnp.broadcast_to(values.astype(F32), (128, COUNT)).astype(BF)
        return lax.dot_general(
            chosen_rows, wide, (((1,), (1,)), ((), ())), preferred_element_type=F32
        )

    slot_line = line[...]
    gslot[...] = (
        16.0 * upright(slot_line >> 4) + upright(slot_line & 15)
    ).astype(jnp.int32) - 1

    only(0, qkv_w[1], out_w[0])
    for copy in m_copies:
        copy.wait()
    total = part[...]
    for dx in STEPS:
        total = total + mrecv[dx].astype(F32)
    ybuf[y] = total.astype(BF)
    y_copies = [
        push(ybuf.at[y], ybuf.at[y], s_my.at[dy], r_my.at[dy], {"y": along(y, dy)})
        for dy in STEPS
    ]
    present = jnp.dot(pick[...], jnp.ones((COUNT, 128), BF), preferred_element_type=F32)
    own_text.wait()
    for copy in text_copies:
        copy.wait()
    for copy in y_copies:
        copy.wait()
    picked = jnp.dot(
        pick[...], ybuf[...].reshape(COUNT, FB), preferred_element_type=F32
    ).astype(BF)
    for group in range(SIDE):
        for part_of in range(2):
            span = slice(group * TOK + part_of * HALF, group * TOK + (part_of + 1) * HALF)
            to = slice(group * HALF, (group + 1) * HALF)
            inside = slice(part_of * HALF, (part_of + 1) * HALF)
            for tile in range(FB // 128):
                cols = slice(tile * 128, (tile + 1) * 128)
                zbuf[part_of, z, to, cols] = jnp.where(
                    present[span, :] > 0.5, picked[span, cols], tbuf[group, inside, cols]
                )

    z_copies, f_copies, x_copies, a_copies, o_copies, e_copies = {}, {}, {}, {}, {}, []

    def spread(layer, part):
        z_copies[layer, part] = {
            dz: push(
                zbuf.at[part, z], zbuf.at[part, z],
                s_z.at[layer, part, dz], r_z.at[layer, part, dz], {"mp": along(z, dz)},
            )
            for dz in (1, 3)
        }

    def times(layer, part, dz):
        zs = behind(z, dz)
        wide = zbuf[part, zs].astype(F32)
        squared = jnp.sum(wide * wide, axis=1, keepdims=True)
        if dz:
            squares[part] += jnp.broadcast_to(squared, (rows, HD))
        else:
            squares[part] = jnp.broadcast_to(squared, (rows, HD))

        @pl.loop(0, PW // 256)
        def _(tile):
            cols = pl.ds(pl.multiple_of(tile * 256, 256), 256)
            product = jnp.dot(
                zbuf[part, zs], w[layer, zs, :, cols], preferred_element_type=F32
            )
            if dz:
                acc[part, :, cols] += product
            else:
                acc[part, :, cols] = product

    def passed(layer, part):
        copies = z_copies[layer, part]
        copies[1].wait()
        zs = behind(z, 1)
        f_copies[layer, part] = [
            push(
                zbuf.at[part, zs, left], zbuf.at[part, zs, left],
                s_z.at[layer, part, 0], r_z.at[layer, part, 0], {"mp": along(z, 1)},
            )
        ]
        copies[3].wait()
        zs = along(z, 1)
        f_copies[layer, part].append(
            push(
                zbuf.at[part, zs, right], zbuf.at[part, zs, right],
                s_z.at[layer, part, 2], r_z.at[layer, part, 2], {"mp": along(z, 3)},
            )
        )

    def own_part(layer, part):
        times(layer, part, 0)

    def project(layer, part):
        times(layer, part, 1)
        times(layer, part, 3)
        for copy in f_copies[layer, part]:
            copy.wait()
        times(layer, part, 2)
        lane = lax.broadcasted_iota(jnp.int32, (HALF, HD), 1)
        copies = []
        for dx in STEPS:
            xt = along(x, dx)
            span = pl.ds(pl.multiple_of(xt * HALF, HALF), HALF)
            psend[part, dx, :, :PW] = acc[part, span, :].astype(BF)
            sq = squares[part, span, :]
            high = sq.astype(BF)
            low = (sq - high.astype(F32)).astype(BF)
            psend[part, dx, :, PW:] = jnp.where(lane < 64, high, low)
            copies.append(
                push(
                    psend.at[part, dx], rbuf.at[part, dx],
                    s_x.at[layer, part, dx], r_x.at[layer, part, dx], {"x": xt},
                )
            )
        x_copies[layer, part] = copies

    def attend(layer, part):
        own = pl.ds(pl.multiple_of(x * HALF, HALF), HALF)
        total = acc[part, own, :]
        sq = squares[part, own, :][:, :1]
        for copy in x_copies[layer, part]:
            copy.wait()
        for dx in STEPS:
            total = total + rbuf[part, dx, :, :PW].astype(F32)
            tail = rbuf[part, dx, :, PW:].astype(F32)
            sq = sq + tail[:, :1] + tail[:, 64:65]
        projected = (total * lax.rsqrt(sq / D + EPSILON)).astype(BF)
        kv[part * HALF : (part + 1) * HALF, :] = projected[:, QW:]
        seen = (part + 1) * HALF
        keys = kv[:seen, :HD]
        values = kv[:seen, HD:]
        queries = jnp.concatenate(
            [projected[:, head * HD : (head + 1) * HD] for head in range(HEADS)], axis=0
        )
        at = iota((HALF, seen), 0) + part * HALF
        key_at = iota((HALF, seen), 1)
        allowed = jnp.where(
            (segments(at, lengths) == segments(key_at, lengths)) & (at >= key_at), 1.0, 0.0
        )
        allowed = jnp.concatenate([allowed] * HEADS, axis=0) > 0.5
        scores = lax.dot_general(
            queries, keys, (((1,), (1,)), ((), ())), preferred_element_type=F32
        ) * (1.0 / math.sqrt(HD))
        scores = jnp.where(allowed, scores, -1e30)
        top = jnp.max(scores, axis=1, keepdims=True)
        weights = jnp.exp(scores - top)
        weights = (weights / jnp.sum(weights, axis=1, keepdims=True)).astype(BF)
        mixed = jnp.dot(weights, values, preferred_element_type=F32).astype(BF)
        for head in range(HEADS):
            abuf[part, x, :, head * HD : (head + 1) * HD] = mixed[
                head * HALF : (head + 1) * HALF, :
            ]
        a_copies[layer, part] = [
            push(
                abuf.at[part, x], abuf.at[part, x],
                s_a.at[layer, part, dx], r_a.at[layer, part, dx], {"x": along(x, dx)},
            )
            for dx in STEPS
        ]

    def output(layer, part):
        for copy in a_copies[layer, part]:
            copy.wait()
        copies = {}

        def send(name, src, dst, dz):
            copies[name] = push(
                src, dst, s_o.at[layer, part, name], r_o.at[layer, part, name],
                {"mp": along(z, dz)},
            )

        for dz in (2, 1, 3, 0):
            zt = along(z, dz)

            @pl.loop(0, FB // 256)
            def _(tile):
                cols = pl.ds(pl.multiple_of(tile * 256, 256), 256)
                osend[part, dz, :, cols] = lax.dot_general(
                    abuf[part].reshape(rows, QW), w[layer, zt, cols, PW:],
                    (((1,), (1,)), ((), ())), preferred_element_type=F32,
                ).astype(BF)

            if dz == 2:
                send(0, osend.at[part, 2, left], orel.at[part, 0], 1)
                send(1, osend.at[part, 2, right], orel.at[part, 1], 3)
            elif dz == 1:
                send(2, osend.at[part, 1, right], orec.at[part, 0, right], 1)
            elif dz == 3:
                send(3, osend.at[part, 3, left], orec.at[part, 1, left], 3)
        o_copies[layer, part] = copies, send

    def relay(layer, part):
        copies, send = o_copies[layer, part]
        copies[0].wait()
        osend[part, 1, left] = (
            osend[part, 1, left].astype(F32) + orel[part, 0].astype(F32)
        ).astype(BF)
        send(4, osend.at[part, 1, left], orec.at[part, 0, left], 1)
        copies[1].wait()
        osend[part, 3, right] = (
            osend[part, 3, right].astype(F32) + orel[part, 1].astype(F32)
        ).astype(BF)
        send(5, osend.at[part, 3, right], orec.at[part, 1, right], 3)

    def finish(layer, part):
        update = osend[part, 0].astype(F32)
        copies, _ = o_copies[layer, part]
        for name in (2, 3, 4, 5):
            copies[name].wait()
        for side in range(2):
            update = update + orec[part, side].astype(F32)
        fresh = (zbuf[part, z].astype(F32) + update).astype(BF)
        if layer == 0:
            zbuf[part, z] = fresh
            return
        osend[part, 0] = fresh
        for dx in STEPS:
            xt = along(x, dx)
            e_copies.append(
                push(
                    osend.at[part, 0, pl.ds(pl.multiple_of(xt * HALF, HALF), HALF), :],
                    obuf.at[x, part],
                    s_e.at[part, dx], r_e.at[part, dx], {"x": xt},
                )
            )
        obuf[x, part] = osend[part, 0, pl.ds(pl.multiple_of(x * HALF, HALF), HALF), :
        ]

    spread(0, 0)
    g_copies, gz_copies = [], []

    def ready_qkv(layer, part):
        only(0, qkv_w[2], out_w[1])
        only(1, last_w[0], qkv_w[3])

    def ready_out(layer, part):
        only(0, out_w[2])
        only(1, out_w[3])

    def pass_last(layer, part):
        only(1, last_w[1])

    def ready_last(layer, part):
        only(1, last_w[2])
        only(0, last_w[3])

    def choose(layer, part):
        own_grads.wait()
        for copy in grad_copies:
            copy.wait()
        for dy in (1, 3, 2, 0):
            yt = along(y, dy)
            wanted = gslot[pl.ds(pl.multiple_of(yt * 64, 64), 64), :1]
            chosen = one_hot(iota((64, SIDE * TOK), 1) == wanted)
            gsend[dy] = jnp.dot(
                chosen, gbuf[...].reshape(SIDE * TOK, width), preferred_element_type=F32
            ).astype(BF)
            if dy:
                g_copies.append(
                    push(gsend.at[dy], grec.at[dy], s_gy.at[dy], r_gy.at[dy], {"y": yt})
                )

    def hand(layer, part):
        for copy in g_copies:
            copy.wait()
        found = gsend[0].astype(F32)
        for dy in STEPS:
            found = found + grec[dy].astype(F32)
        gz[...] = found.astype(BF).reshape(SIDE, UNITS, width)
        for dz in STEPS:
            zt = along(z, dz)
            gz_copies.append(
                push(gz.at[zt], mz.at[z], s_gz.at[dz], r_gz.at[dz], {"mp": zt})
            )
        mz[z] = gz[z]

    for stage, layer, part_at in (
        (ready_qkv, 0, 0),
        (own_part, 0, 0),
        (passed, 0, 0),
        (spread, 0, 1),
        (project, 0, 0),
        (own_part, 0, 1),
        (attend, 0, 0),
        (passed, 0, 1),
        (project, 0, 1),
        (ready_out, 0, 0),
        (output, 0, 0),
        (attend, 0, 1),
        (relay, 0, 0),
        (output, 0, 1),
        (pass_last, 0, 0),
        (finish, 0, 0),
        (spread, 1, 0),
        (relay, 0, 1),
        (choose, 1, 0),
        (ready_last, 1, 0),
        (own_part, 1, 0),
        (finish, 0, 1),
        (passed, 1, 0),
        (spread, 1, 1),
        (project, 1, 0),
        (own_part, 1, 1),
        (attend, 1, 0),
        (passed, 1, 1),
        (project, 1, 1),
        (output, 1, 0),
        (attend, 1, 1),
        (relay, 1, 0),
        (output, 1, 1),
        (hand, 1, 0),
        (finish, 1, 0),
        (relay, 1, 1),
        (finish, 1, 1),
    ):
        stage(layer, part_at)

    for copy in gz_copies:
        copy.wait()
    for block in range(SIDE):
        mg[:, block * width : (block + 1) * width] = mz[block]
    for copy in e_copies:
        copy.wait()
    for block in range(SIDE):
        for part_of in range(2):
            out[part_of * HALF : (part_of + 1) * HALF, block * FB : (block + 1) * FB] = obuf[
                block, part_of
            ]
    merge_w[4]()
    only(0, qkv_w[4], out_w[4])
    only(1, last_w[4])


def shards(*arrays):
    vmem = pl.BlockSpec(memory_space=pltpu.VMEM)
    smem = pl.BlockSpec(memory_space=pltpu.SMEM)
    hbm = pl.BlockSpec(memory_space=pl.ANY)
    dma = pltpu.SemaphoreType.DMA
    rows = SIDE * HALF
    width = arrays[13].shape[1]
    half = arrays[6].shape[0] // 2
    stage = dma((2, 2, SIDE))
    four, plane = dma((SIDE,)), dma((SIDE * SIDE,))
    call = pl.pallas_call(
        whole_kernel,
        out_shape=(
            jax.ShapeDtypeStruct((TOK, SIDE * FB), BF),
            jax.ShapeDtypeStruct((UNITS, SIDE * width), BF),
        ),
        in_specs=[vmem, smem, vmem, hbm, hbm, vmem, hbm, smem, hbm, smem, vmem, hbm, hbm, hbm],
        out_specs=(vmem, vmem),
        scratch_shapes=[
            pltpu.VMEM((SLOTS, VD, TILE), BF),
            pltpu.VMEM((FB, PW), BF),
            pltpu.VMEM((SIDE, 2, half, SIDE * FB), BF),
            pltpu.VMEM((2, SIDE, FB, PW + QW), BF),
            pltpu.VMEM((PATCH, 3 * VD), BF),
            pltpu.VMEM((VH * PATCH, PATCH), F32),
            pltpu.VMEM((VH * PATCH, PATCH), BF),
            pltpu.VMEM((PATCH, VD), F32),
            pltpu.VMEM((PATCH, VD), F32),
            pltpu.VMEM((SIDE, SIDE, UNITS, PADDED), BF),
            pltpu.VMEM((SIDE * SIDE, SIDE, UNITS, PADDED), BF),
            pltpu.VMEM((256, FB), F32),
            pltpu.VMEM((SIDE, 256, FB), BF),
            pltpu.VMEM((SIDE, 256, FB), BF),
            pltpu.VMEM((SIDE, 256, FB), BF),
            pltpu.VMEM((SIDE, TOK, FB), BF),
            pltpu.VMEM((SIDE * TOK, COUNT), BF),
            pltpu.VMEM((1, COUNT), jnp.int32),
            pltpu.VMEM((SIDE * SIDE, 1, COUNT), jnp.int32),
            pltpu.VMEM((SIDE, 1, COUNT), jnp.int32),
            pltpu.VMEM((COUNT, COUNT), BF),
            pltpu.VMEM((1, COUNT), jnp.int32),
            pltpu.VMEM((256, 128), jnp.int32),
            pltpu.VMEM((2, SIDE, rows, FB), BF),
            pltpu.VMEM((2, rows, PW), F32),
            pltpu.VMEM((2, rows, HD), F32),
            pltpu.VMEM((TOK, 2 * HD), BF),
            pltpu.VMEM((2, SIDE, HALF, PT), BF),
            pltpu.VMEM((2, SIDE, HALF, PT), BF),
            pltpu.VMEM((2, SIDE, HALF, QW), BF),
            pltpu.VMEM((2, SIDE, rows, FB), BF),
            pltpu.VMEM((2, 2, rows, FB), BF),
            pltpu.VMEM((2, 2, rows // 2, FB), BF),
            pltpu.VMEM((SIDE, 2, HALF, FB), BF),
            pltpu.VMEM((SIDE, TOK, width), BF),
            pltpu.VMEM((SIDE, 64, width), BF),
            pltpu.VMEM((SIDE, 64, width), BF),
            pltpu.VMEM((SIDE, UNITS, width), BF),
            pltpu.VMEM((SIDE, UNITS, width), BF),
            dma((SLOTS,)), dma((5,)), dma((4, 8)), dma((4, 8)),
            plane, plane, four, four, plane, plane, four, four, four, four, four, four,
            stage, stage, stage, stage, stage, stage, dma((2, 2, 6)), dma((2, 2, 6)),
            dma((2, SIDE)), dma((2, SIDE)),
            four, four, four, four, four, four,
        ],
        compiler_params=pltpu.CompilerParams(
            collective_id=1, has_side_effects=True, vmem_limit_bytes=VMEM_LIMIT
        ),
        name="whole",
    )
    arrays = list(arrays)
    arrays[2] = arrays[2][None, :]
    arrays[5] = arrays[5][None, :]
    return call(*arrays)


def solution(mesh):
    grid = jax.sharding.Mesh(
        mesh.devices.reshape(2, SIDE, SIDE, SIDE), ("section", "y", "x", "mp")
    )
    every = ("section", "y", "x", "mp")
    home = P(("section", "y", "x"), "mp")
    in_specs = (
        P(every, None),
        P(every, None),
        P(),
        P(),
        P(),
        P(),
        P(("y", "x"), "mp"),
        P(every, None),
        home,
        P(("section", "y", "x"), None),
        P("section", None),
        P("section", ("y", "x"), "mp"),
        P("section", ("y", "x"), "mp"),
        home,
    )
    out_specs = (home, P(every, None))
    return jax.shard_map(shards, mesh=grid, in_specs=in_specs, out_specs=out_specs, check_vma=False)
```

time: 271 us -> 249 us (0.919)
  Pallas kernels: 209 us -> 240 us
  local copies, waits for them, and re-layouts: 22.1 us -> 7.47 us
  between operations: 14.2 us -> 0.64 us
  matrix products: 11.4 us -> 0 us
  other arithmetic: 10.2 us -> 0 us
    pallas_call x2 -> x1, Pallas kernels: 209 us -> 240 us  [shards(): return call(*arrays)]
    dot_general x4 -> x0, matrix products: 11.4 us -> none  [the longest x1 6.94 us: vision_rows(): projected = jnp.dot(v_normed, v_qkv, preferred_element_type=F32).astype(BF)]
    reshape x4 -> x0, local copies, waits for them, and re-layouts: 6.89 us -> none  [the longest x1 3.09 us: vision_rows(): projected = projected.reshape(amount, 3, VH, VHD)]
    concatenate x1 -> x0, other arithmetic: 3.24 us -> none  [shards(): w_mine = jnp.concatenate([scaled, wo_t[0]], axis=1)]
    convert_element_type x3 -> x0, other arithmetic: 3.09 us -> none  [the longest x1 1.59 us: shards(): scaled = (w_qkv[0].astype(F32) * gain[:, None]).astype(BF)]
    dynamic_slice x2 -> x0, local copies, waits for them, and re-layouts: 2.89 us -> none  [the longest x1 2.21 us: shards(): lax.dynamic_slice_in_dim(w_merge, section * part, part, 0)]
    slice x2 -> x0, local copies, waits for them, and re-layouts: 2.85 us -> none  [the longest x1 1.97 us: vision_rows(): projected[:, 0]]
    unnamed x20 -> x3, local copies, waits for them, and re-layouts: 5.52 us -> 4.88 us
  transfers between devices with their start and end apart: 3 -> 0, of which waited for: 1 -> 0; matrix products, arithmetic and copies ran while one was open for 13% -> 0% of each run, Pallas kernels for 20% -> 0%
where the time goes in v5:
time: 249 us; the launch traced here: 248 us
  Pallas kernels  240 us (96%)
  local copies, waits for them, and re-layouts  7.47 us (3%)
    pallas_call x1, Pallas kernels, shards(): return call(*arrays)  240 us

profile of v5, /device:TPU:0, one launch (start us, length us, event | category | flops | bytes accessed | tf_op | source)
XLA Modules:
  0.0 248.1 jit_solution(3672018571256395942)
XLA Ops:
  0.6 1.3 broadcast_in_dim.6.v_gain
  1.9 1.3 broadcast_in_dim.7.merge_gain
  3.2 1.3 copy.16.routes
  4.5 240.0 %whole.1 = (bf16[128,2048]{1,0:T(8,128)(2,1)}, bf16[16,8192]{1,0:T(8,128)(2,1)}) custom-call(bf16[64,1280]{1,0:T(8,128)(2,1)} %patches.1, s32[1,3]{1,0:T(1,128)} %units.1, f32[1,1280]{1,0:T(1,128)} %broadcast_in_dim.6.v_gain, bf16[1280,3840]{1,0:T(8,128)(2,1)} %v_qkv.1, bf16[1280,1280]{1,0:T(8,128)(2,1)} %v_out.1, f32[1,1280]{1,0:T(1,128)} %broadcast_in_dim.7.merge_gain, ...), custom_call_target="tpu_custom_call" | custom-call | tf_op jit(solution)/shard_map/whole/pallas_call | solution.py:783
  244.6 1.9 copy.19
  246.4 1.7 copy.20

commit v6 on v5

--- a/solution.py
+++ b/solution.py
@@ -175,18 +175,20 @@
         def begin():
             own_copy(1).start()
             own_copy(3).start()
+            twin_copy(y).start()
 
         def middle():
             own_copy(1).wait()
             up_copy().start()
             own_copy(3).wait()
             down_copy().start()
+            twin_copy(behind(y, 1)).start()
+            twin_copy(along(y, 1)).start()
 
         def end():
             up_copy().wait()
             down_copy().wait()
-            for source in range(SIDE):
-                twin_copy(source).start()
+            twin_copy(along(y, 2)).start()
 
         def taken():
             for source in range(SIDE):
@@ -217,7 +219,8 @@
 
     qkv_w = layer_shard(1, 0, 0, PW)
     out_w = layer_shard(2, 0, PW, QW)
-    last_w = layer_shard(3, 1, 0, PW + QW)
+    last_q = layer_shard(3, 1, 0, PW)
+    last_o = layer_shard(4, 1, PW, QW)
 
     def only(at, *actions):
         @pl.when(section == at)
@@ -244,7 +247,7 @@
             )
         )
     grad_copies = [
-        push(grads, gbuf.at[x], s_g.at[dx], r_g.at[dx], {"x": along(x, dx)}) for dx in STEPS
+        push(grads, gbuf.at[x], s_g.at[dx], r_g.at[dx], {"x": along(x, dx)}) for dx in (1, 3)
     ]
 
     order = iota((PATCH, PATCH), 0)
@@ -393,6 +396,14 @@
     y_copies = [
         push(ybuf.at[y], ybuf.at[y], s_my.at[dy], r_my.at[dy], {"y": along(y, dy)})
         for dy in STEPS
+    ]
+    grad_copies[0].wait()
+    from_left = gbuf.at[behind(x, 1), pl.ds(0, HALF), :]
+    grad_copies[1].wait()
+    from_right = gbuf.at[along(x, 1), pl.ds(HALF, HALF), :]
+    grad_copies = [
+        push(from_left, from_left, s_g.at[0], r_g.at[0], {"x": along(x, 1)}),
+        push(from_right, from_right, s_g.at[2], r_g.at[2], {"x": along(x, 3)}),
     ]
     present = jnp.dot(pick[...], jnp.ones((COUNT, 128), BF), preferred_element_type=F32)
     own_text.wait()
@@ -434,16 +445,13 @@
         else:
             squares[part] = jnp.broadcast_to(squared, (rows, HD))
 
-        @pl.loop(0, PW // 256)
-        def _(tile):
-            cols = pl.ds(pl.multiple_of(tile * 256, 256), 256)
-            product = jnp.dot(
-                zbuf[part, zs], w[layer, zs, :, cols], preferred_element_type=F32
-            )
-            if dz:
-                acc[part, :, cols] += product
-            else:
-                acc[part, :, cols] = product
+        product = jnp.dot(
+            zbuf[part, zs], w[layer, zs, :, :PW], preferred_element_type=F32
+        )
+        if dz:
+            acc[part] += product
+        else:
+            acc[part] = product
 
     def passed(layer, part):
         copies = z_copies[layer, part]
@@ -549,13 +557,10 @@
         for dz in (2, 1, 3, 0):
             zt = along(z, dz)
 
-            @pl.loop(0, FB // 256)
-            def _(tile):
-                cols = pl.ds(pl.multiple_of(tile * 256, 256), 256)
-                osend[part, dz, :, cols] = lax.dot_general(
-                    abuf[part].reshape(rows, QW), w[layer, zt, cols, PW:],
-                    (((1,), (1,)), ((), ())), preferred_element_type=F32,
-                ).astype(BF)
+            osend[part, dz] = lax.dot_general(
+                abuf[part].reshape(rows, QW), w[layer, zt, :, PW:],
+                (((1,), (1,)), ((), ())), preferred_element_type=F32,
+            ).astype(BF)
 
             if dz == 2:
                 send(0, osend.at[part, 2, left], orel.at[part, 0], 1)
@@ -608,18 +613,19 @@
 
     def ready_qkv(layer, part):
         only(0, qkv_w[2], out_w[1])
-        only(1, last_w[0], qkv_w[3])
+        only(1, last_q[0], qkv_w[3])
 
     def ready_out(layer, part):
         only(0, out_w[2])
-        only(1, out_w[3])
-
-    def pass_last(layer, part):
-        only(1, last_w[1])
+        only(1, last_q[1], last_o[0], out_w[3])
 
     def ready_last(layer, part):
-        only(1, last_w[2])
-        only(0, last_w[3])
+        only(1, last_q[2], last_o[1])
+        only(0, last_q[3])
+
+    def ready_end(layer, part):
+        only(1, last_o[2])
+        only(0, last_o[3])
 
     def choose(layer, part):
         own_grads.wait()
@@ -666,11 +672,9 @@
         (attend, 0, 1),
         (relay, 0, 0),
         (output, 0, 1),
-        (pass_last, 0, 0),
         (finish, 0, 0),
         (spread, 1, 0),
         (relay, 0, 1),
-        (choose, 1, 0),
         (ready_last, 1, 0),
         (own_part, 1, 0),
         (finish, 0, 1),
@@ -679,8 +683,10 @@
         (project, 1, 0),
         (own_part, 1, 1),
         (attend, 1, 0),
+        (choose, 1, 0),
         (passed, 1, 1),
         (project, 1, 1),
+        (ready_end, 1, 0),
         (output, 1, 0),
         (attend, 1, 1),
         (relay, 1, 0),
@@ -705,7 +711,7 @@
             ]
     merge_w[4]()
     only(0, qkv_w[4], out_w[4])
-    only(1, last_w[4])
+    only(1, last_q[4], last_o[4])
 
 
 def shards(*arrays):
@@ -766,7 +772,7 @@
             pltpu.VMEM((SIDE, 64, width), BF),
             pltpu.VMEM((SIDE, UNITS, width), BF),
             pltpu.VMEM((SIDE, UNITS, width), BF),
-            dma((SLOTS,)), dma((5,)), dma((4, 8)), dma((4, 8)),
+            dma((SLOTS,)), dma((5,)), dma((5, 8)), dma((5, 8)),
             plane, plane, four, four, plane, plane, four, four, four, four, four, four,
             stage, stage, stage, stage, stage, stage, dma((2, 2, 6)), dma((2, 2, 6)),
             dma((2, SIDE)), dma((2, SIDE)),

time: 249 us -> 221 us (0.89)
  Pallas kernels: 240 us -> 213 us
    pallas_call x1, Pallas kernels: 240 us -> 213 us  [shards(): return call(*arrays)]
where the time goes in v6:
time: 221 us
  Pallas kernels  213 us (96%)
  local copies, waits for them, and re-layouts  7.47 us (3%)
    pallas_call x1, Pallas kernels, shards(): return call(*arrays)  213 us
    unnamed x3, local copies, waits for them, and re-layouts  4.88 us

profile of v6, /device:TPU:0, one launch (start us, length us, event | category | flops | bytes accessed | tf_op | source)
XLA Modules:
  0.0 220.8 jit_solution(6708460787143164018)
XLA Ops:
  0.6 1.3 broadcast_in_dim.6.v_gain
  1.9 1.3 broadcast_in_dim.7.merge_gain
  3.2 1.3 copy.16.routes
  4.5 212.7 %whole.1 = (bf16[128,2048]{1,0:T(8,128)(2,1)}, bf16[16,8192]{1,0:T(8,128)(2,1)}) custom-call(bf16[64,1280]{1,0:T(8,128)(2,1)} %patches.1, s32[1,3]{1,0:T(1,128)} %units.1, f32[1,1280]{1,0:T(1,128)} %broadcast_in_dim.6.v_gain, bf16[1280,3840]{1,0:T(8,128)(2,1)} %v_qkv.1, bf16[1280,1280]{1,0:T(8,128)(2,1)} %v_out.1, f32[1,1280]{1,0:T(1,128)} %broadcast_in_dim.7.merge_gain, ...), custom_call_target="tpu_custom_call" | custom-call | tf_op jit(solution)/shard_map/whole/pallas_call | solution.py:789
  217.3 1.9 copy.19
  219.2 1.7 copy.20

commit v7 on v6

--- a/solution.py
+++ b/solution.py
@@ -253,7 +253,7 @@
     order = iota((PATCH, PATCH), 0)
     swap = one_hot(iota((PATCH, PATCH), 1) == (order & 15) * SIDE + (order >> 4))
     patch = jnp.dot(swap, patches[...], preferred_element_type=F32)
-    normed = layer_norm(patch, v_gain[...]).astype(BF)
+    normed = layer_norm(patch, v_gain[...].reshape(1, VD)).astype(BF)
     for tile in range(15):
         v_tiles[tile].wait()
         v_proj[:, tile * TILE : (tile + 1) * TILE] = jnp.dot(
@@ -296,7 +296,7 @@
             patch[:, cols]
             + jnp.dot(attended, ring[(15 + tile) % SLOTS], preferred_element_type=F32)
         ).astype(BF).astype(F32)
-    merged = layer_norm(v_hidden[...], merge_gain[...])
+    merged = layer_norm(v_hidden[...], merge_gain[...].reshape(1, VD))
     for block in range(SIDE):
         pieces[block, :, :, :PIECE] = merged[:, block * PIECE : (block + 1) * PIECE].astype(BF).reshape(
             SIDE, UNITS, PIECE
@@ -386,7 +386,7 @@
         16.0 * upright(slot_line >> 4) + upright(slot_line & 15)
     ).astype(jnp.int32) - 1
 
-    only(0, qkv_w[1], out_w[0])
+    only(0, qkv_w[1])
     for copy in m_copies:
         copy.wait()
     total = part[...]
@@ -411,6 +411,7 @@
         copy.wait()
     for copy in y_copies:
         copy.wait()
+    only(0, out_w[0])
     picked = jnp.dot(
         pick[...], ybuf[...].reshape(COUNT, FB), preferred_element_type=F32
     ).astype(BF)
@@ -612,12 +613,16 @@
     g_copies, gz_copies = [], []
 
     def ready_qkv(layer, part):
-        only(0, qkv_w[2], out_w[1])
-        only(1, last_q[0], qkv_w[3])
+        only(0, qkv_w[2])
+        only(1, qkv_w[3])
 
     def ready_out(layer, part):
         only(0, out_w[2])
         only(1, last_q[1], last_o[0], out_w[3])
+
+    def pass_out(layer, part):
+        only(0, out_w[1])
+        only(1, last_q[0])
 
     def ready_last(layer, part):
         only(1, last_q[2], last_o[1])
@@ -663,6 +668,7 @@
         (passed, 0, 0),
         (spread, 0, 1),
         (project, 0, 0),
+        (pass_out, 0, 0),
         (own_part, 0, 1),
         (attend, 0, 0),
         (passed, 0, 1),
@@ -783,9 +789,6 @@
         ),
         name="whole",
     )
-    arrays = list(arrays)
-    arrays[2] = arrays[2][None, :]
-    arrays[5] = arrays[5][None, :]
     return call(*arrays)
 
 

time: 221 us -> 198 us (0.90)
  Pallas kernels: 213 us -> 191 us
  local copies, waits for them, and re-layouts: 7.47 us -> 4.88 us
    pallas_call x1, Pallas kernels: 213 us -> 191 us  [shards(): return call(*arrays)]
    broadcast_in_dim x2 -> x0, local copies, waits for them, and re-layouts: 2.59 us -> none  [the longest x1 1.29 us: shards(): arrays[5] = arrays[5][None, :]]
where the time goes in v7:
time: 198 us; the launch traced here: 197 us
  Pallas kernels  191 us (96%)
  local copies, waits for them, and re-layouts  4.88 us (2%)
    pallas_call x1, Pallas kernels, shards(): return call(*arrays)  191 us
    unnamed x3, local copies, waits for them, and re-layouts  4.88 us

profile of v7, /device:TPU:0, one launch (start us, length us, event | category | flops | bytes accessed | tf_op | source)
XLA Modules:
  0.0 197.0 jit_solution(9592651358351131439)
XLA Ops:
  0.6 1.3 copy.16.routes
  2.0 191.5 %whole.1 = (bf16[128,2048]{1,0:T(8,128)(2,1)}, bf16[16,8192]{1,0:T(8,128)(2,1)}) custom-call(bf16[64,1280]{1,0:T(8,128)(2,1)} %patches.1, s32[1,3]{1,0:T(1,128)} %units.1, f32[1280]{0:T(1024)} %v_gain.1, bf16[1280,3840]{1,0:T(8,128)(2,1)} %v_qkv.1, bf16[1280,1280]{1,0:T(8,128)(2,1)} %v_out.1, f32[1280]{0:T(1024)} %merge_gain.1, bf16[320,2048]{1,0:T(8,128)(2,1)} %w_merge.1, ...), custom_call_target="tpu_custom_call" | custom-call | tf_op jit(solution)/shard_map/whole/pallas_call | solution.py:792
  193.4 1.9 copy.19
  195.3 1.7 copy.20

commit v8 on v7

--- a/solution.py
+++ b/solution.py
@@ -246,9 +246,6 @@
                 s_t.at[dx], r_t.at[dx], {"x": xt},
             )
         )
-    grad_copies = [
-        push(grads, gbuf.at[x], s_g.at[dx], r_g.at[dx], {"x": along(x, dx)}) for dx in (1, 3)
-    ]
 
     order = iota((PATCH, PATCH), 0)
     swap = one_hot(iota((PATCH, PATCH), 1) == (order & 15) * SIDE + (order >> 4))
@@ -389,6 +386,9 @@
     only(0, qkv_w[1])
     for copy in m_copies:
         copy.wait()
+    grad_copies = [
+        push(grads, gbuf.at[x], s_g.at[dx], r_g.at[dx], {"x": along(x, dx)}) for dx in (1, 3)
+    ]
     total = part[...]
     for dx in STEPS:
         total = total + mrecv[dx].astype(F32)
@@ -396,14 +396,6 @@
     y_copies = [
         push(ybuf.at[y], ybuf.at[y], s_my.at[dy], r_my.at[dy], {"y": along(y, dy)})
         for dy in STEPS
-    ]
-    grad_copies[0].wait()
-    from_left = gbuf.at[behind(x, 1), pl.ds(0, HALF), :]
-    grad_copies[1].wait()
-    from_right = gbuf.at[along(x, 1), pl.ds(HALF, HALF), :]
-    grad_copies = [
-        push(from_left, from_left, s_g.at[0], r_g.at[0], {"x": along(x, 1)}),
-        push(from_right, from_right, s_g.at[2], r_g.at[2], {"x": along(x, 3)}),
     ]
     present = jnp.dot(pick[...], jnp.ones((COUNT, 128), BF), preferred_element_type=F32)
     own_text.wait()
@@ -610,6 +602,14 @@
         ]
 
     spread(0, 0)
+    grad_copies[0].wait()
+    from_left = gbuf.at[behind(x, 1), pl.ds(0, HALF), :]
+    grad_copies[1].wait()
+    from_right = gbuf.at[along(x, 1), pl.ds(HALF, HALF), :]
+    grad_copies = [
+        push(from_left, from_left, s_g.at[0], r_g.at[0], {"x": along(x, 1)}),
+        push(from_right, from_right, s_g.at[2], r_g.at[2], {"x": along(x, 3)}),
+    ]
     g_copies, gz_copies = [], []
 
     def ready_qkv(layer, part):
@@ -683,8 +683,8 @@
         (relay, 0, 1),
         (ready_last, 1, 0),
         (own_part, 1, 0),
+        (passed, 1, 0),
         (finish, 0, 1),
-        (passed, 1, 0),
         (spread, 1, 1),
         (project, 1, 0),
         (own_part, 1, 1),

time: 198 us -> 195 us (0.985)
  Pallas kernels: 191 us -> 188 us
    pallas_call x1, Pallas kernels: 191 us -> 188 us  [shards(): return call(*arrays)]
where the time goes in v8:
time: 195 us; the launch traced here: 193 us
  Pallas kernels  188 us (96%)
  local copies, waits for them, and re-layouts  4.88 us (3%)
    pallas_call x1, Pallas kernels, shards(): return call(*arrays)  188 us
    unnamed x3, local copies, waits for them, and re-layouts  4.88 us

profile of v8, /device:TPU:0, one launch (start us, length us, event | category | flops | bytes accessed | tf_op | source)
XLA Modules:
  0.0 193.5 jit_solution(18101299570271687817)
XLA Ops:
  0.6 1.3 copy.16.routes
  2.0 187.9 %whole.1 = (bf16[128,2048]{1,0:T(8,128)(2,1)}, bf16[16,8192]{1,0:T(8,128)(2,1)}) custom-call(bf16[64,1280]{1,0:T(8,128)(2,1)} %patches.1, s32[1,3]{1,0:T(1,128)} %units.1, f32[1280]{0:T(1024)} %v_gain.1, bf16[1280,3840]{1,0:T(8,128)(2,1)} %v_qkv.1, bf16[1280,1280]{1,0:T(8,128)(2,1)} %v_out.1, f32[1280]{0:T(1024)} %merge_gain.1, bf16[320,2048]{1,0:T(8,128)(2,1)} %w_merge.1, ...), custom_call_target="tpu_custom_call" | custom-call | tf_op jit(solution)/shard_map/whole/pallas_call | solution.py:792
  189.9 1.9 copy.19
  191.8 1.7 copy.20

commit v9 on v8

--- a/solution.py
+++ b/solution.py
@@ -142,7 +142,7 @@
     base = ((y * SIDE + x) * SIDE + z) * UNITS
     row = jnp.zeros((1, COUNT), jnp.int32)
     for unit in range(UNITS):
-        row = jnp.where(lane == base + unit, routes[unit, 0], row)
+        row = jnp.where(lane == base + unit, routes[0, unit], row)
     placed[...] = row
     rt[x * SIDE + z] = row
 
@@ -789,6 +789,8 @@
         ),
         name="whole",
     )
+    arrays = list(arrays)
+    arrays[7] = arrays[7].reshape(1, UNITS)
     return call(*arrays)
 
 

time: 195 us -> 193 us (0.990)
    unnamed x3 -> x2, local copies, waits for them, and re-layouts: 4.88 us -> 3.55 us
where the time goes in v9:
time: 193 us; the launch traced here: 192 us
  Pallas kernels  188 us (97%)
  local copies, waits for them, and re-layouts  3.55 us (2%)
    pallas_call x1, Pallas kernels, shards(): return call(*arrays)  188 us

profile of v9, /device:TPU:0, one launch (start us, length us, event | category | flops | bytes accessed | tf_op | source)
XLA Modules:
  0.0 192.2 jit_solution(7704545857382937543)
XLA Ops:
  0.6 188.0 %whole.1 = (bf16[128,2048]{1,0:T(8,128)(2,1)}, bf16[16,8192]{1,0:T(8,128)(2,1)}) custom-call(bf16[64,1280]{1,0:T(8,128)(2,1)} %patches.1, s32[1,3]{1,0:T(1,128)} %units.1, f32[1280]{0:T(1024)} %v_gain.1, bf16[1280,3840]{1,0:T(8,128)(2,1)} %v_qkv.1, bf16[1280,1280]{1,0:T(8,128)(2,1)} %v_out.1, f32[1280]{0:T(1024)} %merge_gain.1, bf16[320,2048]{1,0:T(8,128)(2,1)} %w_merge.1, ...), custom_call_target="tpu_custom_call" | custom-call | tf_op jit(solution)/shard_map/whole/pallas_call | solution.py:794
  188.7 1.9 copy.18
  190.5 1.7 copy.19
